TPU v7x, 32 devices: a whole 2x2x4 slice. The times are simulated.
32 devices in a mesh: row: 8 (over y, x, core), col: 4 (over z).
Axes of the slice: x: 2, y: 2, z: 4, core: 2. Of those that a mesh axis runs over, the one named last changes fastest.
Arguments:
- replicas: bfloat16 [2560, 10240], P('row', 'col'), may hold values from -24 to 24
- factor_seeds: int32 [2, 2, 2, 2], replicated, may hold values from 0 to 8190
- edge_counts: int32 [2, 2, 2], replicated, may hold values from 1 to 4
Outputs:
- update: float32 [2560, 10240], P('row', 'col')
All inputs are finite; a program needn't handle non-finite values.
Results may differ from a plain program's by a relative error of at most 0.0003.
Values sent between devices are 32-bit elements; how exact they have to be, the bound alone decides.
No kernel may reach another device: no remote copies, remote signals or barrier semaphores. Data moves between devices by JAX's collectives and lax.ppermute only.
A program may use at most 64 MiB of HBM per device.

v0:
```python
import jax
import jax.numpy as jnp
from jax import lax
from jax.sharding import PartitionSpec as P

ROUNDS = 2
ROW_SHARDS = 4
COL_SHARDS = 2


highest = lax.Precision.HIGHEST
epsilon = 1e-06


def swapped(value, axis, apart):
    return lax.ppermute(value, axis, [(i, i ^ 1 << apart) for i in range(lax.axis_size(axis))])


def from_behind(value, axis, by):
    length = lax.axis_size(axis)
    return lax.ppermute(value, axis, [(i, (i + by) % length) for i in range(length)])


def start_factors(my_seeds, first_column, width):
    column = first_column + jnp.arange(width, dtype=jnp.int32)
    square = column * column % 8191
    residue = (square * (my_seeds[..., None] + 1) + column * 17) % 8191
    return residue.astype(jnp.float32) * (2.0 / 8191.0) - 1.0


def column_total(values):
    values = values + swapped(values, "col", 0)
    return values


def inner_total(values):
    for bit_level in range(ROW_SHARDS.bit_length() - 1):
        values = values + swapped(values, "row", bit_level)
    return values


def projection_total(values):
    for bit_level in range(ROW_SHARDS.bit_length() - 1):
        values = values + swapped(values, "row", bit_level)
    return values


def image_neighbours(stacked):
    from_below = from_behind(stacked[1], "row", -ROW_SHARDS)
    from_above = from_behind(stacked[0], "row", ROW_SHARDS)
    from_right = from_behind(stacked[3], "col", -COL_SHARDS)
    from_left = from_behind(stacked[2], "col", COL_SHARDS)
    return jnp.stack([from_below, from_above, from_right, from_left])


def projection_neighbours(stacked):
    from_below = from_behind(stacked[1], "row", -ROW_SHARDS)
    from_above = from_behind(stacked[0], "row", ROW_SHARDS)
    from_right = from_behind(stacked[3], "col", -COL_SHARDS)
    from_left = from_behind(stacked[2], "col", COL_SHARDS)
    return jnp.stack([from_below, from_above, from_right, from_left])


def orthonormal(values):
    leading = values[:, 0, :]
    second = values[:, 1, :]
    statistics = inner_total(
        jnp.stack(
            [
                jnp.sum(leading * leading, -1),
                jnp.sum(leading * second, -1),
                jnp.sum(second * second, -1),
            ]
        )
    )
    lead_root = jnp.sqrt(statistics[0] + epsilon)
    correlation = statistics[1] / lead_root
    rest_root = jnp.sqrt(statistics[2] - correlation * correlation + epsilon)
    leading = leading / lead_root[:, None]
    second = (second - correlation[:, None] * leading) / rest_root[:, None]
    return jnp.stack([leading, second], 1)


def per_device(replicas, factor_seeds, edge_counts):
    local_rows, local_cols = replicas.shape
    graph_rows, graph_cols = (factor_seeds.shape[0], factor_seeds.shape[1])
    node_row = lax.axis_index("row") // ROW_SHARDS
    node_col = lax.axis_index("col") // COL_SHARDS
    first_column = lax.axis_index("col") % COL_SHARDS * local_cols
    above_row = (node_row + graph_rows - 1) % graph_rows
    left_col = (node_col + graph_cols - 1) % graph_cols
    my_seeds = jnp.stack(
        [
            factor_seeds[node_row, node_col, 0],
            factor_seeds[above_row, node_col, 0],
            factor_seeds[node_row, node_col, 1],
            factor_seeds[node_row, left_col, 1],
        ]
    )
    counts = jnp.stack(
        [
            edge_counts[node_row, node_col, 0],
            edge_counts[above_row, node_col, 0],
            edge_counts[node_row, node_col, 1],
            edge_counts[node_row, left_col, 1],
        ]
    )
    scaling = -(counts.astype(jnp.float32) / 16.0)
    factors = start_factors(my_seeds, first_column, local_cols)
    edge_rows = factors.shape[0] * factors.shape[1]
    update = None
    for round_index in range(ROUNDS):
        flat_factors = factors.reshape(edge_rows, local_cols)
        images = jnp.einsum(
            "fm,km->fk",
            flat_factors,
            replicas,
            precision=highest,
            preferred_element_type=jnp.float32,
        )
        if update is not None:
            images = images + jnp.einsum("fm,km->fk", flat_factors, update, precision=highest)
        images = column_total(images).reshape(factors.shape[0], factors.shape[1], local_rows)
        directions = orthonormal(images - image_neighbours(images))
        flat_directions = directions.reshape(edge_rows, local_rows)
        projections = jnp.einsum(
            "fk,km->fm",
            flat_directions,
            replicas,
            precision=highest,
            preferred_element_type=jnp.float32,
        )
        if update is not None:
            projections = projections + jnp.einsum(
                "fk,km->fm", flat_directions, update, precision=highest
            )
        projections = projections.reshape(factors.shape)
        projections = projection_total(projections)
        factors = projections + projection_neighbours(projections)
        weighted = (scaling[:, None, None] * factors).reshape(edge_rows, local_cols)
        correction = jnp.einsum("fk,fm->km", flat_directions, weighted, precision=highest)
        update = correction if update is None else update + correction
    return update


def solution(mesh):
    in_specs = (P("row", "col"), P(), P())
    out_specs = P("row", "col")
    return jax.shard_map(
        per_device, mesh=mesh, in_specs=in_specs, out_specs=out_specs, check_vma=False
    )
```

profile of v0, /device:TPU:0, one launch (start us, length us, event | category | flops | bytes accessed | tf_op | source)
XLA Modules:
  0.0 85.5 jit_solution(10282834727250718943)
XLA Ops:
  0.0 0.9 fusion.29
  0.9 0.1 add.194
  1.0 0.5 copy-done
  1.5 1.4 %fusion.6 = f32[8,320]{1,0:T(8,128)S(1)} fusion(bf16[320,2560]{1,0:T(8,128)(2,1)S(1)} %copy-done, s32[2560]{0:T(1024)S(1)} %get-tuple-element.46, s32[8]{0:T(128)S(1)} %add.194, s32[2560]{0:T(1024)S(1)} %get-tuple-element.45), kind=kOutput, calls=%fused_computation.11 | convolution fusion | flops 78868480 | bytes 1669152 | tf_op jit(solution)/shard_map/fm,km->fk/dot_general | solution.py:114
  2.9 3.1 %collective-permute-start = (f32[8,320]{1,0:T(8,128)S(1)}, f32[8,320]{1,0:T(8,128)S(1)}, u32[]{:S(2)}, u32[]{:S(2)}) collective-permute-start(f32[8,320]{1,0:T(8,128)S(1)} %fusion.6), channel_id=1, source_target_pairs={{0,1},{1,0},{2,3},{3,2},{4,5},{5,4},{6,7},{7,6},{8,9},{9,8},{10,11... | collective-permute-start | bytes 30728 | tf_op jit(solution)/shard_map/ppermute | solution.py:16
  6.0 1.7 %collective-permute-done = f32[8,320]{1,0:T(8,128)S(1)} collective-permute-done((f32[8,320]{1,0:T(8,128)S(1)}, f32[8,320]{1,0:T(8,128)S(1)}, u32[]{:S(2)}, u32[]{:S(2)}) %collective-permute-start) | collective-permute-done | bytes 10272 | tf_op jit(solution)/shard_map/ppermute | solution.py:16
  7.7 2.0 %collective-permute-start.1 = (f32[2,320]{1,0:T(2,128)S(1)}, f32[2,320]{1,0:T(2,128)S(1)}, u32[]{:S(2)}, u32[]{:S(2)}) collective-permute-start(f32[2,320]{1,0:T(2,128)S(1)} %get-tuple-element.33), channel_id=1, source_target_pairs={{0,16},{4,20},{8,24},{12,28},{16,0},{20,4},{24,8},{28,12},{1,17},{... | collective-permute-start | bytes 7688 | tf_op jit(solution)/shard_map/ppermute | solution.py:21
  9.7 2.6 %collective-permute-start.4 = (f32[2,320]{1,0:T(2,128)S(1)}, f32[2,320]{1,0:T(2,128)S(1)}, u32[]{:S(2)}, u32[]{:S(2)}) collective-permute-start(f32[2,320]{1,0:T(2,128)S(1)} %get-tuple-element.34), channel_id=1, source_target_pairs={{0,2},{1,3},{2,0},{3,1},{4,6},{5,7},{6,4},{7,5},{8,10},{9,11},{10,... | collective-permute-start | bytes 7688 | tf_op jit(solution)/shard_map/ppermute | solution.py:21
  12.3 0.3 collective-permute-start.3
  12.6 0.2 collective-permute-start.2
  12.8 1.4 %collective-permute-done.4 = f32[2,320]{1,0:T(2,128)S(1)} collective-permute-done((f32[2,320]{1,0:T(2,128)S(1)}, f32[2,320]{1,0:T(2,128)S(1)}, u32[]{:S(2)}, u32[]{:S(2)}) %collective-permute-start.4) | collective-permute-done | bytes 2592 | tf_op jit(solution)/shard_map/ppermute | solution.py:21
  14.2 2.6 %collective-permute-done.3 = f32[2,320]{1,0:T(2,128)S(1)} collective-permute-done((f32[2,320]{1,0:T(2,128)S(1)}, f32[2,320]{1,0:T(2,128)S(1)}, u32[]{:S(2)}, u32[]{:S(2)}) %collective-permute-start.3) | collective-permute-done | bytes 2592 | tf_op jit(solution)/shard_map/ppermute | solution.py:21
  16.8 0.1 multiply_reduce_fusion.5
  16.9 0.1 collective-permute-start.5
  17.0 1.1 %collective-permute-done.5 = f32[3,4]{1,0:T(4,128)S(1)} collective-permute-done((f32[3,4]{1,0:T(4,128)S(1)}, f32[3,4]{1,0:T(4,128)S(1)}, u32[]{:S(2)}, u32[]{:S(2)}) %collective-permute-start.5) | collective-permute-done | bytes 80 | tf_op jit(solution)/shard_map/ppermute | solution.py:16
  18.2 1.6 %collective-permute-start.6 = (f32[3,4]{1,0:T(4,128)S(1)}, f32[3,4]{1,0:T(4,128)S(1)}, u32[]{:S(2)}, u32[]{:S(2)}) collective-permute-start(f32[3,4]{1,0:T(4,128)S(1)} %fusion.43), channel_id=1, source_target_pairs={{0,8},{4,12},{8,0},{12,4},{16,24},{20,28},{24,16},{28,20},{1,9},{5... | collective-permute-start | bytes 152 | tf_op jit(solution)/shard_map/ppermute | solution.py:16
  19.7 2.1 %collective-permute-done.6 = f32[3,4]{1,0:T(4,128)S(1)} collective-permute-done((f32[3,4]{1,0:T(4,128)S(1)}, f32[3,4]{1,0:T(4,128)S(1)}, u32[]{:S(2)}, u32[]{:S(2)}) %collective-permute-start.6) | collective-permute-done | bytes 80 | tf_op jit(solution)/shard_map/ppermute | solution.py:16
  21.9 0.1 subtract_divide_fusion.1
  22.0 0.8 fusion.1
  22.8 0.1 collective-permute-start.7
  22.9 1.3 %collective-permute-done.7 = f32[4,2,2560]{2,0,1:T(4,128)S(1)} collective-permute-done((f32[4,2,2560]{2,0,1:T(4,128)S(1)}, f32[4,2,2560]{2,0,1:T(4,128)S(1)}, u32[]{:S(2)}, u32[]{:S(2)}) %collective-permute-start.7) | collective-permute-done | bytes 81952 | tf_op jit(solution)/shard_map/ppermute | solution.py:16
  24.2 1.6 %collective-permute-start.8 = (f32[4,2,2560]{2,0,1:T(4,128)S(1)}, f32[4,2,2560]{2,0,1:T(4,128)S(1)}, u32[]{:S(2)}, u32[]{:S(2)}) collective-permute-start(f32[4,2,2560]{2,0,1:T(4,128)S(1)} %add.203), channel_id=1, source_target_pairs={{0,8},{4,12},{8,0},{12,4},{16,24},{20,28},{24,16},{28,20},{1,9},{5... | collective-permute-start | bytes 245768 | tf_op jit(solution)/shard_map/ppermute | solution.py:16
  25.7 0.6 constant_dynamic-slice_fusion.1
  26.4 2.4 %collective-permute-done.8 = f32[4,2,2560]{2,0,1:T(4,128)S(1)} collective-permute-done((f32[4,2,2560]{2,0,1:T(4,128)S(1)}, f32[4,2,2560]{2,0,1:T(4,128)S(1)}, u32[]{:S(2)}, u32[]{:S(2)}) %collective-permute-start.8) | collective-permute-done | bytes 81952 | tf_op jit(solution)/shard_map/ppermute | solution.py:16
  28.8 0.1 fusion.44
  28.9 2.1 %collective-permute-start.12 = (f32[2,2560]{1,0:T(2,128)S(1)}, f32[2,2560]{1,0:T(2,128)S(1)}, u32[]{:S(2)}, u32[]{:S(2)}) collective-permute-start(f32[2,2560]{1,0:T(2,128)S(1)} %bitcast.92), channel_id=1, source_target_pairs={{0,2},{1,3},{2,0},{3,1},{4,6},{5,7},{6,4},{7,5},{8,10},{9,11},{10,... | collective-permute-start | bytes 61448 | tf_op jit(solution)/shard_map/ppermute | solution.py:21
  31.0 0.5 collective-permute-start.10
  31.5 0.9 %collective-permute-start.11 = (f32[2,2560]{1,0:T(2,128)S(1)}, f32[2,2560]{1,0:T(2,128)S(1)}, u32[]{:S(2)}, u32[]{:S(2)}) collective-permute-start(f32[2,2560]{1,0:T(2,128)S(1)} %bitcast.90), channel_id=1, source_target_pairs={{0,2},{1,3},{2,0},{3,1},{4,6},{5,7},{6,4},{7,5},{8,10},{9,11},{10,... | collective-permute-start | bytes 61448 | tf_op jit(solution)/shard_map/ppermute | solution.py:21
  32.4 1.5 %collective-permute-start.9 = (f32[2,2560]{1,0:T(2,128)S(1)}, f32[2,2560]{1,0:T(2,128)S(1)}, u32[]{:S(2)}, u32[]{:S(2)}) collective-permute-start(f32[2,2560]{1,0:T(2,128)S(1)} %bitcast.89), channel_id=1, source_target_pairs={{0,16},{4,20},{8,24},{12,28},{16,0},{20,4},{24,8},{28,12},{1,17},{... | collective-permute-start | bytes 61448 | tf_op jit(solution)/shard_map/ppermute | solution.py:21
  33.9 2.6 %fusion.34 = f32[4]{0:T(128)S(1)} fusion(s32[1]{0:T(128)} %bitcast.17, s32[1]{0:T(128)} %bitcast.16, s32[1]{0:T(128)} %bitcast.15, s32[1]{0:T(128)} %bitcast.14), kind=kLoop, calls=%fused_computation.78 | loop fusion | flops 24 | bytes 32 | tf_op jit(solution)/shard_map/neg | solution.py:108
  36.7 0.1 broadcast_multiply_fusion
  36.9 2.9 %convolution_bitcast_fusion.1 = f32[320,2560]{1,0:T(8,128)S(1)} fusion(f32[4,2,2560]{2,0,1:T(4,128)S(1)} %get-tuple-element.15, f32[4,1,320]{2,1,0:T(1,128)S(1)} %get-tuple-element.17, f32[4,1,320]{2,1,0:T(1,128)S(1)} %get-tuple-element.18), kind=kOutput, calls=%fused_computation.1 | convolution fusion | flops 78645760 | bytes 3368960 | tf_op jit(solution)/shard_map/fk,fm->km/dot_general | solution.py:141
  39.7 2.7 %fusion.47 = f32[8,320]{1,0:T(8,128)S(1)} fusion(f32[8,2560]{1,0:T(8,128)S(1)} %reshape.237, f32[320,2560]{1,0:T(8,128)S(1)} %convolution_bitcast_fusion.1), kind=kOutput, calls=%fused_computation.99 | convolution fusion | flops 78643200 | bytes 3368960 | tf_op jit(solution)/shard_map/fm,km->fk/dot_general | solution.py:122
  42.5 1.4 %convolution_add_fusion.1 = f32[8,320]{1,0:T(8,128)S(1)} fusion(f32[8,320]{1,0:T(8,128)S(1)} %fusion.47, f32[8,2560]{1,0:T(8,128)S(1)} %reshape.237, bf16[320,2560]{1,0:T(8,128)(2,1)S(1)} %copy-done), kind=kOutput, calls=%fused_computation.6 | convolution fusion | flops 78645760 | bytes 1740800 | tf_op jit(solution)/shard_map/fm,km->fk/dot_general | solution.py:114
  43.9 1.6 %collective-permute-start.13 = (f32[8,320]{1,0:T(8,128)S(1)}, f32[8,320]{1,0:T(8,128)S(1)}, u32[]{:S(2)}, u32[]{:S(2)}) collective-permute-start(f32[8,320]{1,0:T(8,128)S(1)} %convolution_add_fusion.1), channel_id=1, source_target_pairs={{0,1},{1,0},{2,3},{3,2},{4,5},{5,4},{6,7},{7,6},{8,9},{9,8},{10,11... | collective-permute-start | bytes 30728 | tf_op jit(solution)/shard_map/ppermute | solution.py:16
  45.5 2.1 %collective-permute-done.13 = f32[8,320]{1,0:T(8,128)S(1)} collective-permute-done((f32[8,320]{1,0:T(8,128)S(1)}, f32[8,320]{1,0:T(8,128)S(1)}, u32[]{:S(2)}, u32[]{:S(2)}) %collective-permute-start.13) | collective-permute-done | bytes 10272 | tf_op jit(solution)/shard_map/ppermute | solution.py:16
  47.6 1.2 %collective-permute-start.14 = (f32[2,320]{1,0:T(2,128)S(1)}, f32[2,320]{1,0:T(2,128)S(1)}, u32[]{:S(2)}, u32[]{:S(2)}) collective-permute-start(f32[2,320]{1,0:T(2,128)S(1)} %get-tuple-element.29), channel_id=1, source_target_pairs={{0,16},{4,20},{8,24},{12,28},{16,0},{20,4},{24,8},{28,12},{1,17},{... | collective-permute-start | bytes 7688 | tf_op jit(solution)/shard_map/ppermute | solution.py:21
  48.8 2.0 %collective-permute-start.17 = (f32[2,320]{1,0:T(2,128)S(1)}, f32[2,320]{1,0:T(2,128)S(1)}, u32[]{:S(2)}, u32[]{:S(2)}) collective-permute-start(f32[2,320]{1,0:T(2,128)S(1)} %get-tuple-element.30), channel_id=1, source_target_pairs={{0,2},{1,3},{2,0},{3,1},{4,6},{5,7},{6,4},{7,5},{8,10},{9,11},{10,... | collective-permute-start | bytes 7688 | tf_op jit(solution)/shard_map/ppermute | solution.py:21
  50.8 0.9 %collective-permute-start.16 = (f32[2,320]{1,0:T(2,128)S(1)}, f32[2,320]{1,0:T(2,128)S(1)}, u32[]{:S(2)}, u32[]{:S(2)}) collective-permute-start(f32[2,320]{1,0:T(2,128)S(1)} %get-tuple-element.31), channel_id=1, source_target_pairs={{0,2},{1,3},{2,0},{3,1},{4,6},{5,7},{6,4},{7,5},{8,10},{9,11},{10,... | collective-permute-start | bytes 7688 | tf_op jit(solution)/shard_map/ppermute | solution.py:21
  51.7 0.9 %collective-permute-start.15 = (f32[2,320]{1,0:T(2,128)S(1)}, f32[2,320]{1,0:T(2,128)S(1)}, u32[]{:S(2)}, u32[]{:S(2)}) collective-permute-start(f32[2,320]{1,0:T(2,128)S(1)} %get-tuple-element.32), channel_id=1, source_target_pairs={{0,16},{4,20},{8,24},{12,28},{16,0},{20,4},{24,8},{28,12},{1,17},{... | collective-permute-start | bytes 7688 | tf_op jit(solution)/shard_map/ppermute | solution.py:21
  52.6 0.6 collective-permute-done.17
  53.3 2.0 %collective-permute-done.16 = f32[2,320]{1,0:T(2,128)S(1)} collective-permute-done((f32[2,320]{1,0:T(2,128)S(1)}, f32[2,320]{1,0:T(2,128)S(1)}, u32[]{:S(2)}, u32[]{:S(2)}) %collective-permute-start.16) | collective-permute-done | bytes 2592 | tf_op jit(solution)/shard_map/ppermute | solution.py:21
  55.3 0.1 multiply_reduce_fusion.2
  55.5 0.1 collective-permute-start.18
  55.5 1.1 %collective-permute-done.18 = f32[3,4]{1,0:T(4,128)S(1)} collective-permute-done((f32[3,4]{1,0:T(4,128)S(1)}, f32[3,4]{1,0:T(4,128)S(1)}, u32[]{:S(2)}, u32[]{:S(2)}) %collective-permute-start.18) | collective-permute-done | bytes 80 | tf_op jit(solution)/shard_map/ppermute | solution.py:16
  56.7 1.6 %collective-permute-start.19 = (f32[3,4]{1,0:T(4,128)S(1)}, f32[3,4]{1,0:T(4,128)S(1)}, u32[]{:S(2)}, u32[]{:S(2)}) collective-permute-start(f32[3,4]{1,0:T(4,128)S(1)} %fusion.42), channel_id=1, source_target_pairs={{0,8},{4,12},{8,0},{12,4},{16,24},{20,28},{24,16},{28,20},{1,9},{5... | collective-permute-start | bytes 152 | tf_op jit(solution)/shard_map/ppermute | solution.py:16
  58.3 2.1 %collective-permute-done.19 = f32[3,4]{1,0:T(4,128)S(1)} collective-permute-done((f32[3,4]{1,0:T(4,128)S(1)}, f32[3,4]{1,0:T(4,128)S(1)}, u32[]{:S(2)}, u32[]{:S(2)}) %collective-permute-start.19) | collective-permute-done | bytes 80 | tf_op jit(solution)/shard_map/ppermute | solution.py:16
  60.4 0.1 subtract_divide_fusion
  60.5 3.6 %fusion.48 = f32[8,2560]{1,0:T(8,128)S(1)} fusion(f32[8,320]{1,0:T(8,128)S(1)} %reshape.239, f32[320,2560]{1,0:T(8,128)} %copy-done.1), kind=kOutput, calls=%fused_computation.100 | convolution fusion | flops 78643200 | bytes 3368960 | tf_op jit(solution)/shard_map/fk,km->fm/dot_general | solution.py:134
  64.1 0.7 convolution_add_fusion
  64.8 0.1 reshape.240
  64.9 0.1 collective-permute-start.20
  65.0 1.3 %collective-permute-done.20 = f32[4,2,2560]{2,1,0:T(2,128)S(1)} collective-permute-done((f32[4,2,2560]{2,1,0:T(2,128)S(1)}, f32[4,2,2560]{2,1,0:T(2,128)S(1)}, u32[]{:S(2)}, u32[]{:S(2)}) %collective-permute-start.20) | collective-permute-done | bytes 81952 | tf_op jit(solution)/shard_map/ppermute | solution.py:16
  66.3 1.6 %collective-permute-start.21 = (f32[4,2,2560]{2,1,0:T(2,128)S(1)}, f32[4,2,2560]{2,1,0:T(2,128)S(1)}, u32[]{:S(2)}, u32[]{:S(2)}) collective-permute-start(f32[4,2,2560]{2,1,0:T(2,128)S(1)} %add.213), channel_id=1, source_target_pairs={{0,8},{4,12},{8,0},{12,4},{16,24},{20,28},{24,16},{28,20},{1,9},{5... | collective-permute-start | bytes 245768 | tf_op jit(solution)/shard_map/ppermute | solution.py:16
  67.9 3.0 %collective-permute-done.21 = f32[4,2,2560]{2,1,0:T(2,128)S(1)} collective-permute-done((f32[4,2,2560]{2,1,0:T(2,128)S(1)}, f32[4,2,2560]{2,1,0:T(2,128)S(1)}, u32[]{:S(2)}, u32[]{:S(2)}) %collective-permute-start.21) | collective-permute-done | bytes 81952 | tf_op jit(solution)/shard_map/ppermute | solution.py:16
  70.9 1.0 %collective-permute-start.22 = (f32[2,2560]{1,0:T(2,128)S(1)}, f32[2,2560]{1,0:T(2,128)S(1)}, u32[]{:S(2)}, u32[]{:S(2)}) collective-permute-start(f32[2,2560]{1,0:T(2,128)S(1)} %get-tuple-element.21), channel_id=1, source_target_pairs={{0,16},{4,20},{8,24},{12,28},{16,0},{20,4},{24,8},{28,12},{1,17},{... | collective-permute-start | bytes 61448 | tf_op jit(solution)/shard_map/ppermute | solution.py:21
  71.9 2.0 %collective-permute-start.24 = (f32[2,2560]{1,0:T(2,128)S(1)}, f32[2,2560]{1,0:T(2,128)S(1)}, u32[]{:S(2)}, u32[]{:S(2)}) collective-permute-start(f32[2,2560]{1,0:T(2,128)S(1)} %get-tuple-element.23), channel_id=1, source_target_pairs={{0,2},{1,3},{2,0},{3,1},{4,6},{5,7},{6,4},{7,5},{8,10},{9,11},{10,... | collective-permute-start | bytes 61448 | tf_op jit(solution)/shard_map/ppermute | solution.py:21
  73.9 1.1 %collective-permute-start.23 = (f32[2,2560]{1,0:T(2,128)S(1)}, f32[2,2560]{1,0:T(2,128)S(1)}, u32[]{:S(2)}, u32[]{:S(2)}) collective-permute-start(f32[2,2560]{1,0:T(2,128)S(1)} %get-tuple-element.24), channel_id=1, source_target_pairs={{0,16},{4,20},{8,24},{12,28},{16,0},{20,4},{24,8},{28,12},{1,17},{... | collective-permute-start | bytes 61448 | tf_op jit(solution)/shard_map/ppermute | solution.py:21
  75.0 0.9 %collective-permute-start.25 = (f32[2,2560]{1,0:T(2,128)S(1)}, f32[2,2560]{1,0:T(2,128)S(1)}, u32[]{:S(2)}, u32[]{:S(2)}) collective-permute-start(f32[2,2560]{1,0:T(2,128)S(1)} %get-tuple-element.22), channel_id=1, source_target_pairs={{0,2},{1,3},{2,0},{3,1},{4,6},{5,7},{6,4},{7,5},{8,10},{9,11},{10,... | collective-permute-start | bytes 61448 | tf_op jit(solution)/shard_map/ppermute | solution.py:21
  76.0 0.6 collective-permute-done.24
  76.6 1.1 %collective-permute-done.23 = f32[2,2560]{1,0:T(2,128)S(1)} collective-permute-done((f32[2,2560]{1,0:T(2,128)S(1)}, f32[2,2560]{1,0:T(2,128)S(1)}, u32[]{:S(2)}, u32[]{:S(2)}) %collective-permute-start.23) | collective-permute-done | bytes 20512 | tf_op jit(solution)/shard_map/ppermute | solution.py:21
  77.8 2.0 %collective-permute-done.25 = f32[2,2560]{1,0:T(2,128)S(1)} collective-permute-done((f32[2,2560]{1,0:T(2,128)S(1)}, f32[2,2560]{1,0:T(2,128)S(1)}, u32[]{:S(2)}, u32[]{:S(2)}) %collective-permute-start.25) | collective-permute-done | bytes 20512 | tf_op jit(solution)/shard_map/ppermute | solution.py:21
  79.7 0.1 fusion.8
  79.8 5.7 %fusion = f32[320,2560]{1,0:T(8,128)} fusion(f32[320,2560]{1,0:T(8,128)} %copy-done.1, f32[4,2,2560]{2,0,1:T(4,128)S(1)} %fusion.8, f32[4,1,320]{2,1,0:T(1,128)S(1)} %get-tuple-element.11, f32[4,1,320]{2,1,0:T(1,128)S(1)} %get-tuple-element.12), kind=kOutput, calls=%fused_computation.2 | convolution fusion | flops 79464960 | bytes 6645760 | tf_op jit(solution)/shard_map/fk,fm->km/dot_general | solution.py:141
  (56 shorter events, 0.8 us)
Async XLA Ops:
  0.0 1.5 %copy-start = (bf16[320,2560]{1,0:T(8,128)(2,1)S(1)}, bf16[320,2560]{1,0:T(8,128)(2,1)}, u32[]{:S(2)}) copy-start(bf16[320,2560]{1,0:T(8,128)(2,1)} %param.3) | copy-start | bytes 4915204
  1.5 24.2 %copy-start.2 = (s32[2,2,2]{2,1,0:T(2,128)S(1)}, s32[2,2,2]{2,1,0:T(2,128)}, u32[]{:S(2)}) copy-start(s32[2,2,2]{2,1,0:T(2,128)} %param.5) | copy-start | bytes 100
  2.9 4.8 %collective-permute-start = (f32[8,320]{1,0:T(8,128)S(1)}, f32[8,320]{1,0:T(8,128)S(1)}, u32[]{:S(2)}, u32[]{:S(2)}) collective-permute-start(f32[8,320]{1,0:T(8,128)S(1)} %fusion.6), channel_id=1, source_target_pairs={{0,1},{1,0},{2,3},{3,2},{4,5},{5,4},{6,7},{7,6},{8,9},{9,8},{10,11... | collective-permute-start | bytes 30728 | tf_op jit(solution)/shard_map/ppermute | solution.py:16
  7.7 5.2 %collective-permute-start.1 = (f32[2,320]{1,0:T(2,128)S(1)}, f32[2,320]{1,0:T(2,128)S(1)}, u32[]{:S(2)}, u32[]{:S(2)}) collective-permute-start(f32[2,320]{1,0:T(2,128)S(1)} %get-tuple-element.33), channel_id=1, source_target_pairs={{0,16},{4,20},{8,24},{12,28},{16,0},{20,4},{24,8},{28,12},{1,17},{... | collective-permute-start | bytes 7688 | tf_op jit(solution)/shard_map/ppermute | solution.py:21
  9.7 4.5 %collective-permute-start.4 = (f32[2,320]{1,0:T(2,128)S(1)}, f32[2,320]{1,0:T(2,128)S(1)}, u32[]{:S(2)}, u32[]{:S(2)}) collective-permute-start(f32[2,320]{1,0:T(2,128)S(1)} %get-tuple-element.34), channel_id=1, source_target_pairs={{0,2},{1,3},{2,0},{3,1},{4,6},{5,7},{6,4},{7,5},{8,10},{9,11},{10,... | collective-permute-start | bytes 7688 | tf_op jit(solution)/shard_map/ppermute | solution.py:21
  12.3 4.5 %collective-permute-start.3 = (f32[2,320]{1,0:T(2,128)S(1)}, f32[2,320]{1,0:T(2,128)S(1)}, u32[]{:S(2)}, u32[]{:S(2)}) collective-permute-start(f32[2,320]{1,0:T(2,128)S(1)} %get-tuple-element.35), channel_id=1, source_target_pairs={{0,2},{1,3},{2,0},{3,1},{4,6},{5,7},{6,4},{7,5},{8,10},{9,11},{10,... | collective-permute-start | bytes 7688 | tf_op jit(solution)/shard_map/ppermute | solution.py:21
  12.6 4.2 %collective-permute-start.2 = (f32[2,320]{1,0:T(2,128)S(1)}, f32[2,320]{1,0:T(2,128)S(1)}, u32[]{:S(2)}, u32[]{:S(2)}) collective-permute-start(f32[2,320]{1,0:T(2,128)S(1)} %get-tuple-element.36), channel_id=1, source_target_pairs={{0,16},{4,20},{8,24},{12,28},{16,0},{20,4},{24,8},{28,12},{1,17},{... | collective-permute-start | bytes 7688 | tf_op jit(solution)/shard_map/ppermute | solution.py:21
  16.9 1.2 %collective-permute-start.5 = (f32[3,4]{1,0:T(4,128)S(1)}, f32[3,4]{1,0:T(4,128)S(1)}, u32[]{:S(2)}, u32[]{:S(2)}) collective-permute-start(f32[3,4]{1,0:T(4,128)S(1)} %pad_maximum_fusion.2), channel_id=1, source_target_pairs={{0,4},{4,0},{8,12},{12,8},{16,20},{20,16},{24,28},{28,24},{1,5},{5... | collective-permute-start | bytes 152 | tf_op jit(solution)/shard_map/ppermute | solution.py:16
  18.2 3.7 %collective-permute-start.6 = (f32[3,4]{1,0:T(4,128)S(1)}, f32[3,4]{1,0:T(4,128)S(1)}, u32[]{:S(2)}, u32[]{:S(2)}) collective-permute-start(f32[3,4]{1,0:T(4,128)S(1)} %fusion.43), channel_id=1, source_target_pairs={{0,8},{4,12},{8,0},{12,4},{16,24},{20,28},{24,16},{28,20},{1,9},{5... | collective-permute-start | bytes 152 | tf_op jit(solution)/shard_map/ppermute | solution.py:16
  22.8 1.3 %collective-permute-start.7 = (f32[4,2,2560]{2,0,1:T(4,128)S(1)}, f32[4,2,2560]{2,0,1:T(4,128)S(1)}, u32[]{:S(2)}, u32[]{:S(2)}) collective-permute-start(f32[4,2,2560]{2,0,1:T(4,128)S(1)} %fusion.1), channel_id=1, source_target_pairs={{0,4},{4,0},{8,12},{12,8},{16,20},{20,16},{24,28},{28,24},{1,5},{5... | collective-permute-start | bytes 245768 | tf_op jit(solution)/shard_map/ppermute | solution.py:16
  24.2 4.6 %collective-permute-start.8 = (f32[4,2,2560]{2,0,1:T(4,128)S(1)}, f32[4,2,2560]{2,0,1:T(4,128)S(1)}, u32[]{:S(2)}, u32[]{:S(2)}) collective-permute-start(f32[4,2,2560]{2,0,1:T(4,128)S(1)} %add.203), channel_id=1, source_target_pairs={{0,8},{4,12},{8,0},{12,4},{16,24},{20,28},{24,16},{28,20},{1,9},{5... | collective-permute-start | bytes 245768 | tf_op jit(solution)/shard_map/ppermute | solution.py:16
  28.9 7.6 %collective-permute-start.12 = (f32[2,2560]{1,0:T(2,128)S(1)}, f32[2,2560]{1,0:T(2,128)S(1)}, u32[]{:S(2)}, u32[]{:S(2)}) collective-permute-start(f32[2,2560]{1,0:T(2,128)S(1)} %bitcast.92), channel_id=1, source_target_pairs={{0,2},{1,3},{2,0},{3,1},{4,6},{5,7},{6,4},{7,5},{8,10},{9,11},{10,... | collective-permute-start | bytes 61448 | tf_op jit(solution)/shard_map/ppermute | solution.py:21
  31.0 5.6 %collective-permute-start.10 = (f32[2,2560]{1,0:T(2,128)S(1)}, f32[2,2560]{1,0:T(2,128)S(1)}, u32[]{:S(2)}, u32[]{:S(2)}) collective-permute-start(f32[2,2560]{1,0:T(2,128)S(1)} %bitcast.91), channel_id=1, source_target_pairs={{0,16},{4,20},{8,24},{12,28},{16,0},{20,4},{24,8},{28,12},{1,17},{... | collective-permute-start | bytes 61448 | tf_op jit(solution)/shard_map/ppermute | solution.py:21
  31.5 5.1 %collective-permute-start.11 = (f32[2,2560]{1,0:T(2,128)S(1)}, f32[2,2560]{1,0:T(2,128)S(1)}, u32[]{:S(2)}, u32[]{:S(2)}) collective-permute-start(f32[2,2560]{1,0:T(2,128)S(1)} %bitcast.90), channel_id=1, source_target_pairs={{0,2},{1,3},{2,0},{3,1},{4,6},{5,7},{6,4},{7,5},{8,10},{9,11},{10,... | collective-permute-start | bytes 61448 | tf_op jit(solution)/shard_map/ppermute | solution.py:21
  32.4 4.2 %collective-permute-start.9 = (f32[2,2560]{1,0:T(2,128)S(1)}, f32[2,2560]{1,0:T(2,128)S(1)}, u32[]{:S(2)}, u32[]{:S(2)}) collective-permute-start(f32[2,2560]{1,0:T(2,128)S(1)} %bitcast.89), channel_id=1, source_target_pairs={{0,16},{4,20},{8,24},{12,28},{16,0},{20,4},{24,8},{28,12},{1,17},{... | collective-permute-start | bytes 61448 | tf_op jit(solution)/shard_map/ppermute | solution.py:21
  39.7 2.7 %copy-start.1 = (f32[320,2560]{1,0:T(8,128)}, f32[320,2560]{1,0:T(8,128)S(1)}, u32[]{:S(2)}) copy-start(f32[320,2560]{1,0:T(8,128)S(1)} %convolution_bitcast_fusion.1) | copy-start | bytes 9830404
  43.9 3.7 %collective-permute-start.13 = (f32[8,320]{1,0:T(8,128)S(1)}, f32[8,320]{1,0:T(8,128)S(1)}, u32[]{:S(2)}, u32[]{:S(2)}) collective-permute-start(f32[8,320]{1,0:T(8,128)S(1)} %convolution_add_fusion.1), channel_id=1, source_target_pairs={{0,1},{1,0},{2,3},{3,2},{4,5},{5,4},{6,7},{7,6},{8,9},{9,8},{10,11... | collective-permute-start | bytes 30728 | tf_op jit(solution)/shard_map/ppermute | solution.py:16
  47.6 5.0 %collective-permute-start.14 = (f32[2,320]{1,0:T(2,128)S(1)}, f32[2,320]{1,0:T(2,128)S(1)}, u32[]{:S(2)}, u32[]{:S(2)}) collective-permute-start(f32[2,320]{1,0:T(2,128)S(1)} %get-tuple-element.29), channel_id=1, source_target_pairs={{0,16},{4,20},{8,24},{12,28},{16,0},{20,4},{24,8},{28,12},{1,17},{... | collective-permute-start | bytes 7688 | tf_op jit(solution)/shard_map/ppermute | solution.py:21
  48.8 4.5 %collective-permute-start.17 = (f32[2,320]{1,0:T(2,128)S(1)}, f32[2,320]{1,0:T(2,128)S(1)}, u32[]{:S(2)}, u32[]{:S(2)}) collective-permute-start(f32[2,320]{1,0:T(2,128)S(1)} %get-tuple-element.30), channel_id=1, source_target_pairs={{0,2},{1,3},{2,0},{3,1},{4,6},{5,7},{6,4},{7,5},{8,10},{9,11},{10,... | collective-permute-start | bytes 7688 | tf_op jit(solution)/shard_map/ppermute | solution.py:21
  50.8 4.5 %collective-permute-start.16 = (f32[2,320]{1,0:T(2,128)S(1)}, f32[2,320]{1,0:T(2,128)S(1)}, u32[]{:S(2)}, u32[]{:S(2)}) collective-permute-start(f32[2,320]{1,0:T(2,128)S(1)} %get-tuple-element.31), channel_id=1, source_target_pairs={{0,2},{1,3},{2,0},{3,1},{4,6},{5,7},{6,4},{7,5},{8,10},{9,11},{10,... | collective-permute-start | bytes 7688 | tf_op jit(solution)/shard_map/ppermute | solution.py:21
  51.7 3.6 %collective-permute-start.15 = (f32[2,320]{1,0:T(2,128)S(1)}, f32[2,320]{1,0:T(2,128)S(1)}, u32[]{:S(2)}, u32[]{:S(2)}) collective-permute-start(f32[2,320]{1,0:T(2,128)S(1)} %get-tuple-element.32), channel_id=1, source_target_pairs={{0,16},{4,20},{8,24},{12,28},{16,0},{20,4},{24,8},{28,12},{1,17},{... | collective-permute-start | bytes 7688 | tf_op jit(solution)/shard_map/ppermute | solution.py:21
  55.5 1.2 %collective-permute-start.18 = (f32[3,4]{1,0:T(4,128)S(1)}, f32[3,4]{1,0:T(4,128)S(1)}, u32[]{:S(2)}, u32[]{:S(2)}) collective-permute-start(f32[3,4]{1,0:T(4,128)S(1)} %pad_maximum_fusion.3), channel_id=1, source_target_pairs={{0,4},{4,0},{8,12},{12,8},{16,20},{20,16},{24,28},{28,24},{1,5},{5... | collective-permute-start | bytes 152 | tf_op jit(solution)/shard_map/ppermute | solution.py:16
  56.7 3.7 %collective-permute-start.19 = (f32[3,4]{1,0:T(4,128)S(1)}, f32[3,4]{1,0:T(4,128)S(1)}, u32[]{:S(2)}, u32[]{:S(2)}) collective-permute-start(f32[3,4]{1,0:T(4,128)S(1)} %fusion.42), channel_id=1, source_target_pairs={{0,8},{4,12},{8,0},{12,4},{16,24},{20,28},{24,16},{28,20},{1,9},{5... | collective-permute-start | bytes 152 | tf_op jit(solution)/shard_map/ppermute | solution.py:16
  64.9 1.3 %collective-permute-start.20 = (f32[4,2,2560]{2,1,0:T(2,128)S(1)}, f32[4,2,2560]{2,1,0:T(2,128)S(1)}, u32[]{:S(2)}, u32[]{:S(2)}) collective-permute-start(f32[4,2,2560]{2,1,0:T(2,128)S(1)} %reshape.240), channel_id=1, source_target_pairs={{0,4},{4,0},{8,12},{12,8},{16,20},{20,16},{24,28},{28,24},{1,5},{5... | collective-permute-start | bytes 245768 | tf_op jit(solution)/shard_map/ppermute | solution.py:16
  66.3 4.6 %collective-permute-start.21 = (f32[4,2,2560]{2,1,0:T(2,128)S(1)}, f32[4,2,2560]{2,1,0:T(2,128)S(1)}, u32[]{:S(2)}, u32[]{:S(2)}) collective-permute-start(f32[4,2,2560]{2,1,0:T(2,128)S(1)} %add.213), channel_id=1, source_target_pairs={{0,8},{4,12},{8,0},{12,4},{16,24},{20,28},{24,16},{28,20},{1,9},{5... | collective-permute-start | bytes 245768 | tf_op jit(solution)/shard_map/ppermute | solution.py:16
  70.9 5.0 %collective-permute-start.22 = (f32[2,2560]{1,0:T(2,128)S(1)}, f32[2,2560]{1,0:T(2,128)S(1)}, u32[]{:S(2)}, u32[]{:S(2)}) collective-permute-start(f32[2,2560]{1,0:T(2,128)S(1)} %get-tuple-element.21), channel_id=1, source_target_pairs={{0,16},{4,20},{8,24},{12,28},{16,0},{20,4},{24,8},{28,12},{1,17},{... | collective-permute-start | bytes 61448 | tf_op jit(solution)/shard_map/ppermute | solution.py:21
  71.9 4.7 %collective-permute-start.24 = (f32[2,2560]{1,0:T(2,128)S(1)}, f32[2,2560]{1,0:T(2,128)S(1)}, u32[]{:S(2)}, u32[]{:S(2)}) collective-permute-start(f32[2,2560]{1,0:T(2,128)S(1)} %get-tuple-element.23), channel_id=1, source_target_pairs={{0,2},{1,3},{2,0},{3,1},{4,6},{5,7},{6,4},{7,5},{8,10},{9,11},{10,... | collective-permute-start | bytes 61448 | tf_op jit(solution)/shard_map/ppermute | solution.py:21
  73.9 3.8 %collective-permute-start.23 = (f32[2,2560]{1,0:T(2,128)S(1)}, f32[2,2560]{1,0:T(2,128)S(1)}, u32[]{:S(2)}, u32[]{:S(2)}) collective-permute-start(f32[2,2560]{1,0:T(2,128)S(1)} %get-tuple-element.24), channel_id=1, source_target_pairs={{0,16},{4,20},{8,24},{12,28},{16,0},{20,4},{24,8},{28,12},{1,17},{... | collective-permute-start | bytes 61448 | tf_op jit(solution)/shard_map/ppermute | solution.py:21
  75.0 4.7 %collective-permute-start.25 = (f32[2,2560]{1,0:T(2,128)S(1)}, f32[2,2560]{1,0:T(2,128)S(1)}, u32[]{:S(2)}, u32[]{:S(2)}) collective-permute-start(f32[2,2560]{1,0:T(2,128)S(1)} %get-tuple-element.22), channel_id=1, source_target_pairs={{0,2},{1,3},{2,0},{3,1},{4,6},{5,7},{6,4},{7,5},{8,10},{9,11},{10,... | collective-permute-start | bytes 61448 | tf_op jit(solution)/shard_map/ppermute | solution.py:21
where the time goes:
time: 85.7 us; the launch traced here: 85.5 us
  starting transfers between devices  31.4 us (37%)
  waiting for transfers between devices  28.5 us (33%)
  matrix products  19.2 us (22%)
  other arithmetic  3.56 us (4%)
  local copies, waits for them, and re-layouts  2.58 us (3%)
    ppermute x16, starting transfers between devices, from_behind(): lax.ppermute(value, axis, [(i, (i + by) % length) for i in range(length)])  20.2 us
    ppermute x10, waiting for transfers between devices, swapped(): lax.ppermute(value, axis, [(i, i ^ 1 << apart) for i in range(lax.axis_si...  18.2 us
    ppermute x10, starting transfers between devices, swapped(): lax.ppermute(value, axis, [(i, i ^ 1 << apart) for i in range(lax.axis_si...  11.2 us
    ppermute x16, waiting for transfers between devices, from_behind(): lax.ppermute(value, axis, [(i, (i + by) % length) for i in range(length)])  10.3 us
    dot_general x2, matrix products, per_device(): jnp.einsum('fk,fm->km', flat_directions, weighted, precision=highest)  8.55 us
    dot_general x1, matrix products, per_device(): jnp.einsum('fk,km->fm', flat_directions, update, precision=highest)  3.57 us
    dot_general x2, matrix products, per_device(): jnp.einsum('fm,km->fk', flat_factors, replicas, precision=highest, prefer...  2.79 us
    dot_general x1, matrix products, per_device(): jnp.einsum('fm,km->fk', flat_factors, update, precision=highest)  2.71 us
  transfers between devices with their start and end apart: 26, of which 17 were waited for; matrix products, arithmetic and copies ran while one was open for 4% of the time, Pallas kernels for 0%

commit v1 on v0

v1 whole, which is shorter than its diff:
```python
import jax
import jax.numpy as jnp
from jax import lax
from jax.sharding import PartitionSpec as P

ROUNDS = 2
MODULUS_BITS = 13
MODULUS = (1 << MODULUS_BITS) - 1

highest = lax.Precision.HIGHEST
epsilon = 1e-06


def remainder(value):
    value = (value & MODULUS) + (value >> MODULUS_BITS)
    value = (value & MODULUS) + (value >> MODULUS_BITS)
    return jnp.where(value >= MODULUS, value - MODULUS, value)


def start_factors(seeds, first_column, width):
    column = first_column + jnp.arange(width, dtype=jnp.int32)
    square = remainder(column * column)
    residue = remainder(square * (seeds[:, None] + 1) + column * 17)
    return residue.astype(jnp.float32) * (2.0 / MODULUS) - 1.0


def two_terms(values):
    high = lax.reduce_precision(values, 8, 7)
    low = values - high
    return high.astype(jnp.bfloat16), low.astype(jnp.bfloat16)


def times_exact(values, exact, dimension):
    count = values.shape[0]
    terms = jnp.concatenate(two_terms(values), 0)
    product = lax.dot_general(
        terms, exact, (((1,), (dimension,)), ((), ())), preferred_element_type=jnp.float32
    )
    return product[:count] + product[count:]


def small_product(left, right, left_dim, right_dim):
    return lax.dot_general(
        left,
        right,
        (((left_dim,), (right_dim,)), ((), ())),
        precision=highest,
        preferred_element_type=jnp.float32,
    )


class Layout:
    def __init__(self, graph_rows, graph_cols):
        self.rows, self.cols = lax.axis_size("row"), lax.axis_size("col")
        self.nodes = (graph_rows, graph_cols)
        self.shards = (self.rows // graph_rows, self.cols // graph_cols)

    def exchange(self, value, target):
        pairs = []
        for r in range(self.rows):
            for c in range(self.cols):
                tr, tc = target(r, c)
                pairs.append((r * self.cols + c, tr * self.cols + tc))
        return lax.ppermute(value, ("row", "col"), pairs)

    def row_swap(self, value, bit):
        return self.exchange(value, lambda r, c: (r ^ 1 << bit, c))

    def col_swap(self, value, bit):
        return self.exchange(value, lambda r, c: (r, c ^ 1 << bit))

    def step(self, half, by):
        def target(r, c):
            if (r & 1) == half:
                return (r + by * self.shards[0]) % self.rows, c
            return r, (c + by * self.shards[1]) % self.cols

        return target

    def neighbours(self, value, half):
        if self.nodes == (2, 2):
            other = self.exchange(value, self.step(half, 1))
            return jnp.concatenate([other[2:], other[:2]], 0)
        after = self.exchange(value[2:], self.step(half, -1))
        before = self.exchange(value[:2], self.step(half, 1))
        return jnp.concatenate([after, before], 0)


def per_device(replicas, factor_seeds, edge_counts):
    local_rows, local_cols = replicas.shape
    graph_rows, graph_cols = factor_seeds.shape[:2]
    layout = Layout(graph_rows, graph_cols)
    row_index, col_index = lax.axis_index("row"), lax.axis_index("col")
    node_row, node_col = row_index // layout.shards[0], col_index // layout.shards[1]
    first_column = col_index % layout.shards[1] * local_cols
    above_row = (node_row + graph_rows - 1) % graph_rows
    left_col = (node_col + graph_cols - 1) % graph_cols
    first_half = row_index & 1
    edges = []
    for half in range(2):
        along_col = first_half ^ half
        edges.append((node_row, node_col, along_col))
        edges.append(
            (
                jnp.where(along_col == 0, above_row, node_row),
                jnp.where(along_col == 0, node_col, left_col),
                along_col,
            )
        )
    seeds = jnp.concatenate([factor_seeds[r, c, a] for r, c, a in edges])
    counts = jnp.stack([edge_counts[r, c, a] for r, c, a in edges])
    scaling = -(counts.astype(jnp.float32) / 16.0)

    factors = start_factors(seeds, first_column, local_cols)
    lefts, rights = [], []
    for round_index in range(ROUNDS):
        images = times_exact(factors, replicas, 1)
        for left, right in zip(lefts, rights):
            images = images + small_product(small_product(factors, right, 1, 1), left, 1, 0)
        for bit in range(layout.shards[1].bit_length() - 1):
            images = images + layout.col_swap(images, bit)
        others = [layout.neighbours(images[4 * half : 4 * half + 4], half) for half in range(2)]
        left = images - jnp.concatenate(others, 0)

        projections = times_exact(left, replicas, 0)
        for earlier, right in zip(lefts, rights):
            projections = projections + small_product(small_product(left, earlier, 1, 1), right, 1, 0)
        pairs = left.reshape(4, 2, local_rows)
        inner = jnp.sum(pairs[:, :, None] * pairs[:, None, :], -1).reshape(8, 2)
        packed = jnp.concatenate([projections, jnp.pad(inner, ((0, 0), (0, 126)))], 1)
        total = packed[:4] + layout.row_swap(packed[4:], 0)
        for bit in range(1, layout.shards[0].bit_length() - 1):
            total = total + layout.row_swap(total, bit)
        total = total + layout.neighbours(total, 0)
        total = jnp.concatenate([total, layout.row_swap(total, 0)], 0)

        raw = total[:, :local_cols].reshape(4, 2, local_cols)
        gram = 0.5 * total[:, local_cols : local_cols + 2].reshape(4, 2, 2)
        lead_square = gram[:, 0, 0] + epsilon
        lead_root = jnp.sqrt(lead_square)
        correlation = gram[:, 0, 1] / lead_root
        rest = gram[:, 1, 1] - correlation * correlation * (1.0 + epsilon / lead_square)
        rest_root = jnp.sqrt(jnp.maximum(rest, 0.0) + epsilon)
        first = (1.0 / lead_root)[:, None]
        mixed = (-correlation / (lead_root * rest_root))[:, None]
        second = (1.0 / rest_root)[:, None]
        lead_factor = first * raw[:, 0]
        rest_factor = second * raw[:, 1] + mixed * raw[:, 0]
        factors = jnp.stack([lead_factor, rest_factor], 1).reshape(8, local_cols)
        weight = scaling[:, None]
        right = jnp.stack(
            [weight * (first * lead_factor + mixed * rest_factor), weight * second * rest_factor], 1
        ).reshape(8, local_cols)
        lefts.append(left)
        rights.append(right)

    left_high, left_low = two_terms(jnp.concatenate(lefts, 0))
    right_high, right_low = two_terms(jnp.concatenate(rights, 0))
    return lax.dot_general(
        jnp.concatenate([left_high, left_low, left_high], 0),
        jnp.concatenate([right_high, right_high, right_low], 0),
        (((0,), (0,)), ((), ())),
        preferred_element_type=jnp.float32,
    )


def solution(mesh):
    in_specs = (P("row", "col"), P(), P())
    out_specs = P("row", "col")
    return jax.shard_map(
        per_device, mesh=mesh, in_specs=in_specs, out_specs=out_specs, check_vma=False
    )
```

time: 85.7 us -> 53.4 us (0.62)
  matrix products: 19.2 us -> 4.84 us
  starting transfers between devices: 31.4 us -> 18.4 us
  waiting for transfers between devices: 28.5 us -> 22.2 us
  other arithmetic: 3.56 us -> 4.45 us
    dot_general x8 -> x9, matrix products: 19.2 us -> 4.84 us  [the longest x1 2.31 us: per_device(): lax.dot_general(jnp.concatenate([left_high, left_low, left_high], 0), jnp...]
    ppermute x26 -> x14, starting transfers between devices: 31.4 us -> 18.4 us  [exchange(): return lax.ppermute(value, ('row', 'col'), pairs)]
    ppermute x26 -> x14, waiting for transfers between devices: 28.5 us -> 22.2 us  [exchange(): return lax.ppermute(value, ('row', 'col'), pairs)]
    mul x2 -> x7, other arithmetic: 0.2 us -> 2.91 us  [the longest x3 2.69 us: per_device(): weight * second * rest_factor]
    neg x1 -> x0, other arithmetic: 2.6 us -> none  [per_device(): scaling = -(counts.astype(jnp.float32) / 16.0)]
    concatenate x0 -> x2, local copies, waits for them, and re-layouts: none -> 0.87 us  [the longest x1 0.86 us: per_device(): seeds = jnp.concatenate([factor_seeds[r, c, a] for r, c, a in edges])]
    another operation x9 -> x3, local copies, waits for them, and re-layouts: 1 us -> 0.13 us  [the longest x2 0.09 us: per_device(): jnp.stack([weight * (first * lead_factor + mixed * rest_factor), weight *...]
  transfers between devices with their start and end apart: 26 -> 14, of which waited for: 17 -> 13; matrix products, arithmetic and copies ran while one was open for 4% -> 1% of each run, Pallas kernels for 0% -> 0%
where the time goes in v1:
time: 53.4 us; the launch traced here: 53.2 us
  waiting for transfers between devices  22.2 us (42%)
  starting transfers between devices  18.4 us (34%)
  matrix products  4.84 us (9%)
  other arithmetic  4.45 us (8%)
  local copies, waits for them, and re-layouts  2.96 us (6%)
    ppermute x14, waiting for transfers between devices, exchange(): return lax.ppermute(value, ('row', 'col'), pairs)  22.2 us
    ppermute x14, starting transfers between devices, exchange(): return lax.ppermute(value, ('row', 'col'), pairs)  18.4 us
    mul x3, other arithmetic, per_device(): weight * second * rest_factor  2.69 us
    dot_general x1, matrix products, per_device(): lax.dot_general(jnp.concatenate([left_high, left_low, left_high], 0), jnp...  2.31 us
    dot_general x4, matrix products, times_exact(): lax.dot_general(terms, exact, (((1,), (dimension,)), ((), ())), preferred...  1.8 us
  transfers between devices with their start and end apart: 14, of which 13 were waited for; matrix products, arithmetic and copies ran while one was open for 1% of the time, Pallas kernels for 0%

profile of v1, /device:TPU:0, one launch (start us, length us, event | category | flops | bytes accessed | tf_op | source)
XLA Modules:
  0.0 53.2 jit_solution(16891325608075550041)
XLA Ops:
  0.1 0.9 %fusion.39 = (s32[2]{0:T(128)S(1)}, s32[2]{0:T(128)S(1)}, s32[2]{0:T(128)S(1)}, s32[2]{0:T(128)S(1)}) fusion(s32[2,2,2,2]{3,2,1,0:T(2,128)} %param.4, s32[]{:T(128)S(6)} %select_n.89, s32[]{:T(128)S(6)} %select_n.91, s32[]{:T(128)S(6)} %select_n.92, s32[]{:T(128)S(6)} %select_n.95, s32[]{:T(128)S(6)} %select_n.98, s32[]{:T(128)S(6)} %select_n.101, ...), kind=kLoop, calls=%fused_computation.98 | loop fusion | bytes 96 | tf_op jit(solution)/shard_map/concatenate | solution.py:110
  0.9 0.1 add_add_fusion
  1.0 0.1 reduce-precision_convert_fusion.2
  1.1 0.4 copy-done
  1.5 0.5 fusion.12
  2.0 3.1 %collective-permute-start = (f32[8,320]{1,0:T(8,128)S(1)}, f32[8,320]{1,0:T(8,128)S(1)}, u32[]{:S(2)}, u32[]{:S(2)}) collective-permute-start(f32[8,320]{1,0:T(8,128)S(1)} %slice_add_fusion.5), channel_id=1, source_target_pairs={{0,1},{1,0},{2,3},{3,2},{4,5},{5,4},{6,7},{7,6},{8,9},{9,8},{10,11... | collective-permute-start | bytes 30728 | tf_op jit(solution)/shard_map/ppermute | solution.py:64
  5.1 1.7 %collective-permute-done = f32[8,320]{1,0:T(8,128)S(1)} collective-permute-done((f32[8,320]{1,0:T(8,128)S(1)}, f32[8,320]{1,0:T(8,128)S(1)}, u32[]{:S(2)}, u32[]{:S(2)}) %collective-permute-start) | collective-permute-done | bytes 10272 | tf_op jit(solution)/shard_map/ppermute | solution.py:64
  6.8 2.0 %collective-permute-start.1 = (f32[4,320]{1,0:T(4,128)S(1)}, f32[4,320]{1,0:T(4,128)S(1)}, u32[]{:S(2)}, u32[]{:S(2)}) collective-permute-start(f32[4,320]{1,0:T(4,128)S(1)} %get-tuple-element.43), channel_id=1, source_target_pairs={{0,16},{1,17},{2,18},{3,19},{4,6},{5,7},{6,4},{7,5},{8,24},{9,25},... | collective-permute-start | bytes 15368 | tf_op jit(solution)/shard_map/ppermute | solution.py:64
  8.9 2.6 %collective-permute-start.2 = (f32[4,320]{1,0:T(4,128)S(1)}, f32[4,320]{1,0:T(4,128)S(1)}, u32[]{:S(2)}, u32[]{:S(2)}) collective-permute-start(f32[4,320]{1,0:T(4,128)S(1)} %get-tuple-element.44), channel_id=1, source_target_pairs={{0,2},{1,3},{2,0},{3,1},{4,20},{5,21},{6,22},{7,23},{8,10},{9,11},... | collective-permute-start | bytes 15368 | tf_op jit(solution)/shard_map/ppermute | solution.py:64
  11.5 1.9 %collective-permute-done.2 = f32[4,320]{1,0:T(4,128)S(1)} collective-permute-done((f32[4,320]{1,0:T(4,128)S(1)}, f32[4,320]{1,0:T(4,128)S(1)}, u32[]{:S(2)}, u32[]{:S(2)}) %collective-permute-start.2) | collective-permute-done | bytes 5152 | tf_op jit(solution)/shard_map/ppermute | solution.py:64
  13.5 0.1 multiply_reduce_fusion.1
  13.6 0.1 copy.49
  13.7 0.3 fusion.30
  14.1 0.1 collective-permute-start.3
  14.1 1.2 %collective-permute-done.3 = f32[4,2688]{1,0:T(4,128)S(1)} collective-permute-done((f32[4,2688]{1,0:T(4,128)S(1)}, f32[4,2688]{1,0:T(4,128)S(1)}, u32[]{:S(2)}, u32[]{:S(2)}) %collective-permute-start.3) | collective-permute-done | bytes 43040 | tf_op jit(solution)/shard_map/ppermute | solution.py:64
  15.4 1.6 %collective-permute-start.4 = (f32[4,2688]{1,0:T(4,128)S(1)}, f32[4,2688]{1,0:T(4,128)S(1)}, u32[]{:S(2)}, u32[]{:S(2)}) collective-permute-start(f32[4,2688]{1,0:T(4,128)S(1)} %slice_add_fusion.3), channel_id=1, source_target_pairs={{0,8},{1,9},{2,10},{3,11},{4,12},{5,13},{6,14},{7,15},{8,0},{9,1},... | collective-permute-start | bytes 129032 | tf_op jit(solution)/shard_map/ppermute | solution.py:64
  16.9 2.5 %collective-permute-done.4 = f32[4,2688]{1,0:T(4,128)S(1)} collective-permute-done((f32[4,2688]{1,0:T(4,128)S(1)}, f32[4,2688]{1,0:T(4,128)S(1)}, u32[]{:S(2)}, u32[]{:S(2)}) %collective-permute-start.4) | collective-permute-done | bytes 43040 | tf_op jit(solution)/shard_map/ppermute | solution.py:64
  19.5 0.2 collective-permute-start.5
  19.7 3.9 %collective-permute-done.5 = f32[4,2688]{1,0:T(4,128)S(1)} collective-permute-done((f32[4,2688]{1,0:T(4,128)S(1)}, f32[4,2688]{1,0:T(4,128)S(1)}, u32[]{:S(2)}, u32[]{:S(2)}) %collective-permute-start.5) | collective-permute-done | bytes 43040 | tf_op jit(solution)/shard_map/ppermute | solution.py:64
  23.6 0.1 collective-permute-start.6
  23.7 0.7 %fusion.66 = (s32[1,1,1]{2,1,0:T(1,128)}, s32[1,1,1]{2,1,0:T(1,128)}, s32[1,1,1]{2,1,0:T(1,128)}, s32[1,1,1]{2,1,0:T(1,128)}) fusion(s32[2,2,2]{2,1,0:T(2,128)S(1)} %copy-done.1, s32[]{:T(128)S(6)} %select_n.89, s32[]{:T(128)S(6)} %select_n.91, s32[]{:T(128)S(6)} %select_n.92, s32[]{:T(128)S(6)} %select_n.95, s32[]{:T(128)S(6)} %select_n.98, ...), kind=kLoop, calls=%fused_computation.129 | loop fusion | bytes 64 | tf_op jit(solution)/shard_map/dynamic_slice | solution.py:111
  24.4 0.5 collective-permute-done.6
  24.9 0.1 reshape.426
  25.0 0.1 fusion.55
  25.1 0.1 fusion.65
  25.1 0.1 reduce.2
  25.3 0.1 reduce.1
  25.4 0.2 rsqrt_reduce_fusion.1
  25.5 2.6 %fusion.52 = (f32[4]{0:T(128)S(1)}, f32[4]{0:T(128)S(1)}, f32[4]{0:T(128)S(1)}, f32[4]{0:T(128)S(1)}) fusion(s32[1]{0:T(128)} %bitcast.9, s32[1]{0:T(128)} %bitcast.8, s32[1]{0:T(128)} %bitcast.7, s32[1]{0:T(128)} %bitcast.6, f32[4]{0:T(128)S(1)} %reduce.1, f32[4]{0:T(128)S(1)} %get-tuple-element.9, f32[4]{0:T(128)S(1)} %reduce.2, ...), kind=kLoop, calls=%fused_computation.116 | loop fusion | flops 88 | bytes 160 | tf_op jit(solution)/shard_map/mul | solution.py:152
  28.1 0.1 add_multiply_fusion.1
  28.2 0.1 broadcast_multiply_fusion.1
  28.4 0.1 reshape.427
  28.5 0.1 reshape.428
  28.6 0.2 fusion.67
  28.9 0.6 %fusion.16 = f32[16,320]{1,0:T(8,128)S(1)} fusion(bf16[320,2560]{1,0:T(8,128)(2,1)S(1)} %copy-done, bf16[8,2560]{1,0:T(8,128)(2,1)S(1)} %get-tuple-element.29, bf16[8,2560]{1,0:T(8,128)(2,1)S(1)} %get-tuple-element.28), kind=kOutput, calls=%fused_computation.33 | convolution fusion | flops 26378240 | bytes 1740800 | tf_op jit(solution)/shard_map/dot_general | solution.py:36
  29.4 0.1 convolution_add_fusion.1
  29.6 1.6 %collective-permute-start.7 = (f32[8,320]{1,0:T(8,128)S(1)}, f32[8,320]{1,0:T(8,128)S(1)}, u32[]{:S(2)}, u32[]{:S(2)}) collective-permute-start(f32[8,320]{1,0:T(8,128)S(1)} %convolution_add_fusion.1), channel_id=1, source_target_pairs={{0,1},{1,0},{2,3},{3,2},{4,5},{5,4},{6,7},{7,6},{8,9},{9,8},{10,11... | collective-permute-start | bytes 30728 | tf_op jit(solution)/shard_map/ppermute | solution.py:64
  31.2 2.1 %collective-permute-done.7 = f32[8,320]{1,0:T(8,128)S(1)} collective-permute-done((f32[8,320]{1,0:T(8,128)S(1)}, f32[8,320]{1,0:T(8,128)S(1)}, u32[]{:S(2)}, u32[]{:S(2)}) %collective-permute-start.7) | collective-permute-done | bytes 10272 | tf_op jit(solution)/shard_map/ppermute | solution.py:64
  33.3 0.2 collective-permute-start.8
  33.6 2.9 %collective-permute-start.9 = (f32[4,320]{1,0:T(4,128)S(1)}, f32[4,320]{1,0:T(4,128)S(1)}, u32[]{:S(2)}, u32[]{:S(2)}) collective-permute-start(f32[4,320]{1,0:T(4,128)S(1)} %get-tuple-element.42), channel_id=1, source_target_pairs={{0,2},{1,3},{2,0},{3,1},{4,20},{5,21},{6,22},{7,23},{8,10},{9,11},... | collective-permute-start | bytes 15368 | tf_op jit(solution)/shard_map/ppermute | solution.py:64
  36.5 0.5 %collective-permute-done.8 = f32[4,320]{1,0:T(4,128)S(1)} collective-permute-done((f32[4,320]{1,0:T(4,128)S(1)}, f32[4,320]{1,0:T(4,128)S(1)}, u32[]{:S(2)}, u32[]{:S(2)}) %collective-permute-start.8) | collective-permute-done | bytes 5152 | tf_op jit(solution)/shard_map/ppermute | solution.py:64
  37.0 1.1 %collective-permute-done.9 = f32[4,320]{1,0:T(4,128)S(1)} collective-permute-done((f32[4,320]{1,0:T(4,128)S(1)}, f32[4,320]{1,0:T(4,128)S(1)}, u32[]{:S(2)}, u32[]{:S(2)}) %collective-permute-start.9) | collective-permute-done | bytes 5152 | tf_op jit(solution)/shard_map/ppermute | solution.py:64
  38.1 0.1 fusion.68
  38.3 0.1 multiply_reduce_fusion
  38.4 0.1 copy.51
  38.5 0.3 fusion.34
  38.8 0.2 convolution_add_fusion
  39.1 0.1 collective-permute-start.10
  39.2 1.2 %collective-permute-done.10 = f32[4,2688]{1,0:T(4,128)S(1)} collective-permute-done((f32[4,2688]{1,0:T(4,128)S(1)}, f32[4,2688]{1,0:T(4,128)S(1)}, u32[]{:S(2)}, u32[]{:S(2)}) %collective-permute-start.10) | collective-permute-done | bytes 43040 | tf_op jit(solution)/shard_map/ppermute | solution.py:64
  40.4 1.9 %collective-permute-start.11 = (f32[4,2688]{1,0:T(4,128)S(1)}, f32[4,2688]{1,0:T(4,128)S(1)}, u32[]{:S(2)}, u32[]{:S(2)}) collective-permute-start(f32[4,2688]{1,0:T(4,128)S(1)} %slice_add_fusion.2), channel_id=1, source_target_pairs={{0,8},{1,9},{2,10},{3,11},{4,12},{5,13},{6,14},{7,15},{8,0},{9,1},... | collective-permute-start | bytes 129032 | tf_op jit(solution)/shard_map/ppermute | solution.py:64
  42.3 2.2 %collective-permute-done.11 = f32[4,2688]{1,0:T(4,128)S(1)} collective-permute-done((f32[4,2688]{1,0:T(4,128)S(1)}, f32[4,2688]{1,0:T(4,128)S(1)}, u32[]{:S(2)}, u32[]{:S(2)}) %collective-permute-start.11) | collective-permute-done | bytes 43040 | tf_op jit(solution)/shard_map/ppermute | solution.py:64
  44.5 1.9 %collective-permute-start.12 = (f32[4,2688]{1,0:T(4,128)S(1)}, f32[4,2688]{1,0:T(4,128)S(1)}, u32[]{:S(2)}, u32[]{:S(2)}) collective-permute-start(f32[4,2688]{1,0:T(4,128)S(1)} %add.318), channel_id=1, source_target_pairs={{0,16},{1,17},{2,18},{3,19},{4,6},{5,7},{6,4},{7,5},{8,24},{9,25},... | collective-permute-start | bytes 129032 | tf_op jit(solution)/shard_map/ppermute | solution.py:64
  46.4 2.2 %collective-permute-done.12 = f32[4,2688]{1,0:T(4,128)S(1)} collective-permute-done((f32[4,2688]{1,0:T(4,128)S(1)}, f32[4,2688]{1,0:T(4,128)S(1)}, u32[]{:S(2)}, u32[]{:S(2)}) %collective-permute-start.12) | collective-permute-done | bytes 43040 | tf_op jit(solution)/shard_map/ppermute | solution.py:64
  48.6 0.1 collective-permute-start.13
  48.7 1.2 %collective-permute-done.13 = f32[4,2688]{1,0:T(4,128)S(1)} collective-permute-done((f32[4,2688]{1,0:T(4,128)S(1)}, f32[4,2688]{1,0:T(4,128)S(1)}, u32[]{:S(2)}, u32[]{:S(2)}) %collective-permute-start.13) | collective-permute-done | bytes 43040 | tf_op jit(solution)/shard_map/ppermute | solution.py:64
  49.9 0.1 reshape.430
  50.0 0.1 fusion.54
  50.1 0.1 fusion.64
  50.2 0.1 reduce.6
  50.3 0.1 reduce.8
  50.4 0.2 sqrt_reduce_fusion
  50.6 0.1 add_multiply_fusion
  50.8 0.1 reshape.431
  50.9 2.3 %fusion = f32[320,2560]{1,0:T(8,128)} fusion(bf16[16,2560]{1,0:T(8,128)(2,1)S(1)} %get-tuple-element.23, bf16[16,2560]{1,0:T(8,128)(2,1)S(1)} %get-tuple-element.22, bf16[16,320]{1,0:T(8,128)(2,1)S(1)} %get-tuple-element.40, bf16[16,320]{1,0:T(8,128)(2,1)S(1)} %get-tuple-element.39), kind=kOutput, calls=%fused_computation.2 | convolution fusion | flops 79472640 | bytes 3461120 | tf_op jit(solution)/shard_map/dot_general | solution.py:159
  (51 shorter events, 0.7 us)
Async XLA Ops:
  0.0 1.5 %copy-start = (bf16[320,2560]{1,0:T(8,128)(2,1)S(1)}, bf16[320,2560]{1,0:T(8,128)(2,1)}, u32[]{:S(2)}) copy-start(bf16[320,2560]{1,0:T(8,128)(2,1)} %param.3) | copy-start | bytes 4915204
  2.0 21.7 %copy-start.1 = (s32[2,2,2]{2,1,0:T(2,128)S(1)}, s32[2,2,2]{2,1,0:T(2,128)}, u32[]{:S(2)}) copy-start(s32[2,2,2]{2,1,0:T(2,128)} %param.5) | copy-start | bytes 100
  2.0 4.8 %collective-permute-start = (f32[8,320]{1,0:T(8,128)S(1)}, f32[8,320]{1,0:T(8,128)S(1)}, u32[]{:S(2)}, u32[]{:S(2)}) collective-permute-start(f32[8,320]{1,0:T(8,128)S(1)} %slice_add_fusion.5), channel_id=1, source_target_pairs={{0,1},{1,0},{2,3},{3,2},{4,5},{5,4},{6,7},{7,6},{8,9},{9,8},{10,11... | collective-permute-start | bytes 30728 | tf_op jit(solution)/shard_map/ppermute | solution.py:64
  6.8 4.6 %collective-permute-start.1 = (f32[4,320]{1,0:T(4,128)S(1)}, f32[4,320]{1,0:T(4,128)S(1)}, u32[]{:S(2)}, u32[]{:S(2)}) collective-permute-start(f32[4,320]{1,0:T(4,128)S(1)} %get-tuple-element.43), channel_id=1, source_target_pairs={{0,16},{1,17},{2,18},{3,19},{4,6},{5,7},{6,4},{7,5},{8,24},{9,25},... | collective-permute-start | bytes 15368 | tf_op jit(solution)/shard_map/ppermute | solution.py:64
  8.9 4.5 %collective-permute-start.2 = (f32[4,320]{1,0:T(4,128)S(1)}, f32[4,320]{1,0:T(4,128)S(1)}, u32[]{:S(2)}, u32[]{:S(2)}) collective-permute-start(f32[4,320]{1,0:T(4,128)S(1)} %get-tuple-element.44), channel_id=1, source_target_pairs={{0,2},{1,3},{2,0},{3,1},{4,20},{5,21},{6,22},{7,23},{8,10},{9,11},... | collective-permute-start | bytes 15368 | tf_op jit(solution)/shard_map/ppermute | solution.py:64
  14.1 1.3 %collective-permute-start.3 = (f32[4,2688]{1,0:T(4,128)S(1)}, f32[4,2688]{1,0:T(4,128)S(1)}, u32[]{:S(2)}, u32[]{:S(2)}) collective-permute-start(f32[4,2688]{1,0:T(4,128)S(1)} %slice.181), channel_id=1, source_target_pairs={{0,4},{1,5},{2,6},{3,7},{4,0},{5,1},{6,2},{7,3},{8,12},{9,13},{10,... | collective-permute-start | bytes 129032 | tf_op jit(solution)/shard_map/ppermute | solution.py:64
  15.4 4.1 %collective-permute-start.4 = (f32[4,2688]{1,0:T(4,128)S(1)}, f32[4,2688]{1,0:T(4,128)S(1)}, u32[]{:S(2)}, u32[]{:S(2)}) collective-permute-start(f32[4,2688]{1,0:T(4,128)S(1)} %slice_add_fusion.3), channel_id=1, source_target_pairs={{0,8},{1,9},{2,10},{3,11},{4,12},{5,13},{6,14},{7,15},{8,0},{9,1},... | collective-permute-start | bytes 129032 | tf_op jit(solution)/shard_map/ppermute | solution.py:64
  19.5 4.1 %collective-permute-start.5 = (f32[4,2688]{1,0:T(4,128)S(1)}, f32[4,2688]{1,0:T(4,128)S(1)}, u32[]{:S(2)}, u32[]{:S(2)}) collective-permute-start(f32[4,2688]{1,0:T(4,128)S(1)} %add.303), channel_id=1, source_target_pairs={{0,16},{1,17},{2,18},{3,19},{4,6},{5,7},{6,4},{7,5},{8,24},{9,25},... | collective-permute-start | bytes 129032 | tf_op jit(solution)/shard_map/ppermute | solution.py:64
  23.6 1.3 %collective-permute-start.6 = (f32[4,2688]{1,0:T(4,128)S(1)}, f32[4,2688]{1,0:T(4,128)S(1)}, u32[]{:S(2)}, u32[]{:S(2)}) collective-permute-start(f32[4,2688]{1,0:T(4,128)S(1)} %maximum_add_fusion), channel_id=1, source_target_pairs={{0,4},{1,5},{2,6},{3,7},{4,0},{5,1},{6,2},{7,3},{8,12},{9,13},{10,... | collective-permute-start | bytes 129032 | tf_op jit(solution)/shard_map/ppermute | solution.py:64
  29.6 3.7 %collective-permute-start.7 = (f32[8,320]{1,0:T(8,128)S(1)}, f32[8,320]{1,0:T(8,128)S(1)}, u32[]{:S(2)}, u32[]{:S(2)}) collective-permute-start(f32[8,320]{1,0:T(8,128)S(1)} %convolution_add_fusion.1), channel_id=1, source_target_pairs={{0,1},{1,0},{2,3},{3,2},{4,5},{5,4},{6,7},{7,6},{8,9},{9,8},{10,11... | collective-permute-start | bytes 30728 | tf_op jit(solution)/shard_map/ppermute | solution.py:64
  33.3 3.7 %collective-permute-start.8 = (f32[4,320]{1,0:T(4,128)S(1)}, f32[4,320]{1,0:T(4,128)S(1)}, u32[]{:S(2)}, u32[]{:S(2)}) collective-permute-start(f32[4,320]{1,0:T(4,128)S(1)} %get-tuple-element.41), channel_id=1, source_target_pairs={{0,16},{1,17},{2,18},{3,19},{4,6},{5,7},{6,4},{7,5},{8,24},{9,25},... | collective-permute-start | bytes 15368 | tf_op jit(solution)/shard_map/ppermute | solution.py:64
  33.6 4.5 %collective-permute-start.9 = (f32[4,320]{1,0:T(4,128)S(1)}, f32[4,320]{1,0:T(4,128)S(1)}, u32[]{:S(2)}, u32[]{:S(2)}) collective-permute-start(f32[4,320]{1,0:T(4,128)S(1)} %get-tuple-element.42), channel_id=1, source_target_pairs={{0,2},{1,3},{2,0},{3,1},{4,20},{5,21},{6,22},{7,23},{8,10},{9,11},... | collective-permute-start | bytes 15368 | tf_op jit(solution)/shard_map/ppermute | solution.py:64
  39.1 1.3 %collective-permute-start.10 = (f32[4,2688]{1,0:T(4,128)S(1)}, f32[4,2688]{1,0:T(4,128)S(1)}, u32[]{:S(2)}, u32[]{:S(2)}) collective-permute-start(f32[4,2688]{1,0:T(4,128)S(1)} %slice.200), channel_id=1, source_target_pairs={{0,4},{1,5},{2,6},{3,7},{4,0},{5,1},{6,2},{7,3},{8,12},{9,13},{10,... | collective-permute-start | bytes 129032 | tf_op jit(solution)/shard_map/ppermute | solution.py:64
  40.4 4.1 %collective-permute-start.11 = (f32[4,2688]{1,0:T(4,128)S(1)}, f32[4,2688]{1,0:T(4,128)S(1)}, u32[]{:S(2)}, u32[]{:S(2)}) collective-permute-start(f32[4,2688]{1,0:T(4,128)S(1)} %slice_add_fusion.2), channel_id=1, source_target_pairs={{0,8},{1,9},{2,10},{3,11},{4,12},{5,13},{6,14},{7,15},{8,0},{9,1},... | collective-permute-start | bytes 129032 | tf_op jit(solution)/shard_map/ppermute | solution.py:64
  44.5 4.1 %collective-permute-start.12 = (f32[4,2688]{1,0:T(4,128)S(1)}, f32[4,2688]{1,0:T(4,128)S(1)}, u32[]{:S(2)}, u32[]{:S(2)}) collective-permute-start(f32[4,2688]{1,0:T(4,128)S(1)} %add.318), channel_id=1, source_target_pairs={{0,16},{1,17},{2,18},{3,19},{4,6},{5,7},{6,4},{7,5},{8,24},{9,25},... | collective-permute-start | bytes 129032 | tf_op jit(solution)/shard_map/ppermute | solution.py:64
  48.6 1.3 %collective-permute-start.13 = (f32[4,2688]{1,0:T(4,128)S(1)}, f32[4,2688]{1,0:T(4,128)S(1)}, u32[]{:S(2)}, u32[]{:S(2)}) collective-permute-start(f32[4,2688]{1,0:T(4,128)S(1)} %maximum_add_fusion.1), channel_id=1, source_target_pairs={{0,4},{1,5},{2,6},{3,7},{4,0},{5,1},{6,2},{7,3},{8,12},{9,13},{10,... | collective-permute-start | bytes 129032 | tf_op jit(solution)/shard_map/ppermute | solution.py:64

commit v2 on v1

v2 whole, which is shorter than its diff:
```python
import functools

import jax
import jax.numpy as jnp
from jax import lax
from jax.experimental import pallas as pl
from jax.experimental.pallas import tpu as pltpu
from jax.sharding import PartitionSpec as P

MODULUS_BITS = 13
MODULUS = (1 << MODULUS_BITS) - 1
LANES = 128
CHUNKS = 5

epsilon = 1e-06
over_last = (((1,), (1,)), ((), ()))
over_inner = (((1,), (0,)), ((), ()))
over_first = (((0,), (0,)), ((), ()))


class Layout:
    def __init__(self, graph_rows, graph_cols):
        self.rows, self.cols = lax.axis_size("row"), lax.axis_size("col")
        self.nodes = (graph_rows, graph_cols)
        self.shards = (self.rows // graph_rows, self.cols // graph_cols)

    def exchange(self, value, target):
        pairs = []
        for r in range(self.rows):
            for c in range(self.cols):
                tr, tc = target(r, c)
                pairs.append((r * self.cols + c, tr * self.cols + tc))
        return lax.ppermute(value, ("row", "col"), pairs)

    def row_swap(self, value, bit):
        return self.exchange(value, lambda r, c: (r ^ 1 << bit, c))

    def col_swap(self, value, bit):
        return self.exchange(value, lambda r, c: (r, c ^ 1 << bit))

    def step(self, half, by):
        def target(r, c):
            if (r & 1) == half:
                return (r + by * self.shards[0]) % self.rows, c
            return r, (c + by * self.shards[1]) % self.cols

        return target

    def neighbours(self, value, half):
        if self.nodes == (2, 2):
            return self.exchange(value, self.step(half, 1))
        after = self.exchange(value[2:], self.step(half, -1))
        before = self.exchange(value[:2], self.step(half, 1))
        return jnp.concatenate([after, before], 0)

    def edges(self):
        row_index, col_index = lax.axis_index("row"), lax.axis_index("col")
        node = (row_index // self.shards[0], col_index // self.shards[1])
        found = []
        for half in range(2):
            along_col = (row_index & 1) ^ half
            for slot in range(2):
                owner = []
                for axis in range(2):
                    if self.nodes == (2, 2):
                        mine = slot
                    else:
                        mine = lax.rem(node[axis] + self.nodes[axis] - slot, self.nodes[axis])
                    owner.append(jnp.where(along_col == axis, mine, node[axis]))
                found.append((owner[0], owner[1], along_col))
        return found

    def first_column(self, width):
        return lax.rem(lax.axis_index("col"), self.shards[1]) * width


def stacked(values):
    high = values.astype(jnp.bfloat16).astype(jnp.float32)
    return jnp.concatenate([high, values - high], 0).astype(jnp.bfloat16)


def folded(product):
    half = product.shape[0] // 2
    return product[:half] + product[half:]


def dot(left, right, dims):
    return lax.dot_general(left, right, dims, preferred_element_type=jnp.float32)


def full_product(left, right, dims):
    high = right.astype(jnp.bfloat16)
    low = (right - high.astype(jnp.float32)).astype(jnp.bfloat16)
    terms = stacked(left)
    return folded(dot(terms, high, dims) + dot(terms, low, dims))


def remainder(value):
    value = (value & MODULUS) + (value >> MODULUS_BITS)
    value = (value & MODULUS) + (value >> MODULUS_BITS)
    return jnp.where(value >= MODULUS, value - MODULUS, value)


def row_values(scalars, width):
    rows = lax.broadcasted_iota(jnp.int32, (len(scalars), width), 0)
    values = jnp.full((len(scalars), width), scalars[0], jnp.int32)
    for k in range(1, len(scalars)):
        values = jnp.where(rows == k, scalars[k], values)
    return values


def first_kernel(layout, seeds_ref, counts_ref, replicas_ref, images_ref, scaling_ref):
    edges = layout.edges()
    seeds = row_values([seeds_ref[r, c, a, k] for r, c, a in edges for k in range(2)], LANES)
    counts = row_values([counts_ref[r, c, a] for r, c, a in edges for k in range(2)], LANES)
    scaling_ref[...] = -(counts.astype(jnp.float32) / 16.0)
    width = replicas_ref.shape[1]
    column = layout.first_column(width) + lax.broadcasted_iota(jnp.int32, (8, width), 1)
    square = remainder(column * column)
    residue = remainder(square * (seeds[:, :1] + 1) + column * 17)
    factors = residue.astype(jnp.float32) * (2.0 / MODULUS) - 1.0
    images_ref[...] = folded(dot(stacked(factors), replicas_ref[...], over_last))


def project_kernel(has_update, images_ref, first_ref, second_ref, replicas_ref, *refs):
    if has_update:
        earlier_ref, right_ref, left_ref, keep_ref, send_ref = refs
    else:
        left_ref, keep_ref, send_ref = refs
    left_ref[0:4] = images_ref[0:4] - first_ref[...]
    left_ref[4:8] = images_ref[4:8] - second_ref[...]
    left = left_ref[...]
    width = replicas_ref.shape[1]
    projections = folded(dot(stacked(left), replicas_ref[...], over_inner))
    if has_update:
        cross = full_product(left, earlier_ref[...], over_last)
        projections = projections + full_product(cross, right_ref[...], over_inner)
    rows = lax.broadcasted_iota(jnp.int32, left.shape, 0)
    partner = jnp.where(rows % 2 == 0, pltpu.roll(left, 7, 0), pltpu.roll(left, 1, 0))
    norm = jnp.sum(left * left, 1, keepdims=True)
    inner = jnp.sum(left * partner, 1, keepdims=True)
    lanes = lax.broadcasted_iota(jnp.int32, (8, LANES), 1)
    tail = jnp.where(lanes == 0, norm, inner)
    keep_ref[:, :width] = projections[0:4]
    send_ref[:, :width] = projections[4:8]
    keep_ref[:, width:] = tail[0:4]
    send_ref[:, width:] = tail[4:8]


def orthonormal_factors(mine_ref, other_ref, scaling, total_ref):
    total_ref[0:4] = mine_ref[...]
    total_ref[4:8] = other_ref[...]
    width = total_ref.shape[1] - LANES
    raw = total_ref[:, :width]
    tail = 0.5 * total_ref[:, width:]
    even = lax.broadcasted_iota(jnp.int32, (8, LANES), 0) % 2 == 0
    after, before = pltpu.roll(tail, 7, 0), pltpu.roll(tail, 1, 0)
    lead = jnp.where(even, tail, before)[:, 0:1]
    rest = jnp.where(even, after, tail)[:, 0:1]
    inner = tail[:, 1:2]
    lead_square = lead + epsilon
    lead_root = jnp.sqrt(lead_square)
    correlation = inner / lead_root
    rest = rest - correlation * correlation * (1.0 + epsilon / lead_square)
    rest_root = jnp.sqrt(jnp.maximum(rest, 0.0) + epsilon)
    mixed = -correlation / (lead_root * rest_root)
    even = even[:, 0:1]
    own = jnp.where(even, 1.0 / lead_root, 1.0 / rest_root)
    factors = own * raw + jnp.where(even, 0.0, mixed) * pltpu.roll(raw, 1, 0)
    right = own * factors + jnp.where(even, mixed, 0.0) * pltpu.roll(factors, 7, 0)
    return factors, scaling * right


def images_kernel(mine_ref, other_ref, scaling_ref, left_ref, replicas_ref, images_ref, right_ref, total_ref):
    factors, right = orthonormal_factors(mine_ref, other_ref, scaling_ref[:, 0:1], total_ref)
    right_ref[...] = right
    images = folded(dot(stacked(factors), replicas_ref[...], over_last))
    cross = full_product(factors, right, over_last)
    images_ref[...] = images + full_product(cross, left_ref[...], over_inner)


def update_kernel(
    mine_ref, other_ref, scaling_ref, first_ref, second_ref, right_ref, out_ref, total_ref, terms_ref, block_ref, sems
):
    _, right = orthonormal_factors(mine_ref, other_ref, scaling_ref[:, 0:1], total_ref)
    lefts = jnp.concatenate([first_ref[...], second_ref[...]], 0)
    left_high = lefts.astype(jnp.bfloat16).astype(jnp.float32)
    left_terms = jnp.concatenate([left_high, lefts - left_high, left_high], 0).astype(jnp.bfloat16)
    rights = jnp.concatenate([right_ref[...], right], 0)
    right_high = rights.astype(jnp.bfloat16).astype(jnp.float32)
    terms_ref[...] = jnp.concatenate([right_high, right_high, rights - right_high], 0).astype(
        jnp.bfloat16
    )
    size = block_ref.shape[2]
    copies = []
    for k in range(block_ref.shape[0]):
        columns = pl.ds(k * size, size)
        block_ref[k] = dot(left_terms, terms_ref[:, columns], over_first)
        copies.append(pltpu.make_async_copy(block_ref.at[k], out_ref.at[:, columns], sems.at[k]))
        copies[-1].start()
    for copy in copies:
        copy.wait()


vmem = pl.BlockSpec(memory_space=pltpu.VMEM)
smem = pl.BlockSpec(memory_space=pltpu.SMEM)


def call(kernel, outs, *args, in_specs=None, out_specs=None, scratch=()):
    return pl.pallas_call(
        kernel,
        out_shape=[jax.ShapeDtypeStruct(shape, jnp.float32) for shape in outs],
        in_specs=in_specs or [vmem] * len(args),
        out_specs=out_specs or [vmem] * len(outs),
        scratch_shapes=list(scratch),
        compiler_params=pltpu.CompilerParams(vmem_limit_bytes=16 << 20),
    )(*args)


def per_device(replicas, factor_seeds, edge_counts):
    height, width = replicas.shape
    packed = width + LANES
    layout = Layout(*factor_seeds.shape[:2])
    total_scratch = pltpu.VMEM((8, packed), jnp.float32)

    def reduced(images):
        for bit in range(layout.shards[1].bit_length() - 1):
            images = images + layout.col_swap(images, bit)
        return images, layout.neighbours(images[:4], 0), layout.neighbours(images[4:], 1)

    def summed(keep, send):
        total = keep + layout.row_swap(send, 0)
        for bit in range(1, layout.shards[0].bit_length() - 1):
            total = total + layout.row_swap(total, bit)
        total = total + layout.neighbours(total, 0)
        return total, layout.row_swap(total, 0)

    images, scaling = call(
        functools.partial(first_kernel, layout),
        [(8, height), (8, LANES)],
        factor_seeds,
        edge_counts,
        replicas,
        in_specs=[smem, smem, vmem],
    )
    left_one, keep, send = call(
        functools.partial(project_kernel, False),
        [(8, height), (4, packed), (4, packed)],
        *reduced(images),
        replicas,
    )
    mine, other = summed(keep, send)
    images, right_one = call(
        images_kernel,
        [(8, height), (8, width)],
        mine,
        other,
        scaling,
        left_one,
        replicas,
        scratch=[total_scratch],
    )
    left_two, keep, send = call(
        functools.partial(project_kernel, True),
        [(8, height), (4, packed), (4, packed)],
        *reduced(images),
        replicas,
        left_one,
        right_one,
    )
    mine, other = summed(keep, send)
    (update,) = call(
        update_kernel,
        [(height, width)],
        mine,
        other,
        scaling,
        left_one,
        left_two,
        right_one,
        out_specs=[pl.BlockSpec(memory_space=pl.ANY)],
        scratch=[
            total_scratch,
            pltpu.VMEM((48, width), jnp.bfloat16),
            pltpu.VMEM((CHUNKS, height, width // CHUNKS), jnp.float32),
            pltpu.SemaphoreType.DMA((CHUNKS,)),
        ],
    )
    return update


def solution(mesh):
    in_specs = (P("row", "col"), P(), P())
    out_specs = P("row", "col")
    return jax.shard_map(
        per_device, mesh=mesh, in_specs=in_specs, out_specs=out_specs, check_vma=False
    )
```

time: 53.4 us -> 51.2 us (0.959)
  Pallas kernels: 0 us -> 5.32 us
  matrix products: 4.84 us -> 0 us
  other arithmetic: 4.45 us -> 0.08 us
  local copies, waits for them, and re-layouts: 2.96 us -> 4.24 us
  waiting for transfers between devices: 22.2 us -> 22.9 us
    pallas_call x0 -> x5, Pallas kernels: none -> 5.32 us  [call(): pl.pallas_call(kernel, out_shape=[jax.ShapeDtypeStruct(shape, jnp.float32...]
    dot_general x9 -> x0, matrix products: 4.84 us -> none  [the longest x1 2.31 us: per_device(): lax.dot_general(jnp.concatenate([left_high, left_low, left_high], 0), jnp...]
    unnamed x5 -> x8, local copies, waits for them, and re-layouts: 0.38 us -> 4.23 us
    mul x7 -> x0, other arithmetic: 2.91 us -> none  [the longest x3 2.69 us: per_device(): weight * second * rest_factor]
    concatenate x2 -> x0, local copies, waits for them, and re-layouts: 0.87 us -> none  [the longest x1 0.86 us: per_device(): seeds = jnp.concatenate([factor_seeds[r, c, a] for r, c, a in edges])]
    ppermute x14, waiting for transfers between devices: 22.2 us -> 22.9 us  [exchange(): return lax.ppermute(value, ('row', 'col'), pairs)]
    dynamic_slice x1 -> x0, local copies, waits for them, and re-layouts: 0.67 us -> none  [per_device(): counts = jnp.stack([edge_counts[r, c, a] for r, c, a in edges])]
  transfers between devices with their start and end apart: 14 -> 14, of which waited for: 13 -> 13; matrix products, arithmetic and copies ran while one was open for 1% -> 0% of each run, Pallas kernels for 0% -> 0%
where the time goes in v2:
time: 51.2 us; the launch traced here: 51 us
  waiting for transfers between devices  22.9 us (45%)
  starting transfers between devices  18.4 us (36%)
  Pallas kernels  5.32 us (10%)
  local copies, waits for them, and re-layouts  4.24 us (8%)
    ppermute x14, waiting for transfers between devices, exchange(): return lax.ppermute(value, ('row', 'col'), pairs)  22.9 us
    ppermute x14, starting transfers between devices, exchange(): return lax.ppermute(value, ('row', 'col'), pairs)  18.4 us
    pallas_call x5, Pallas kernels, call(): pl.pallas_call(kernel, out_shape=[jax.ShapeDtypeStruct(shape, jnp.float32...  5.32 us
    unnamed x8, local copies, waits for them, and re-layouts  4.23 us
  transfers between devices with their start and end apart: 14, of which 13 were waited for; matrix products, arithmetic and copies ran while one was open for 0% of the time, Pallas kernels for 0%

profile of v2, /device:TPU:0, one launch (start us, length us, event | category | flops | bytes accessed | tf_op | source)
XLA Modules:
  0.0 51.0 jit_solution(9336690188484140754)
XLA Ops:
  0.0 0.0 copy-start
  0.0 1.4 %copy-done = bf16[320,2560]{1,0:T(8,128)(2,1)S(1)} copy-done((bf16[320,2560]{1,0:T(8,128)(2,1)S(1)}, bf16[320,2560]{1,0:T(8,128)(2,1)}, u32[]{:S(2)}) %copy-start) | copy-done | bytes 1638424
  1.4 0.0 copy-start.2
  1.4 0.7 %copy-done.2 = s32[2,2,2,2]{3,2,1,0:T(2,128)S(1)} copy-done((s32[2,2,2,2]{3,2,1,0:T(2,128)S(1)}, s32[2,2,2,2]{3,2,1,0:T(2,128)}, u32[]{:S(2)}) %copy-start.2) | copy-done | bytes 88
  2.1 0.0 copy-start.3
  2.1 0.7 %copy-done.3 = s32[2,2,2]{2,1,0:T(2,128)S(1)} copy-done((s32[2,2,2]{2,1,0:T(2,128)S(1)}, s32[2,2,2]{2,1,0:T(2,128)}, u32[]{:S(2)}) %copy-start.3) | copy-done | bytes 56
  2.8 1.1 %shard_map.37 = (f32[8,320]{1,0:T(8,128)S(1)}, f32[8,128]{1,0:T(8,128)S(1)}) custom-call(s32[2,2,2,2]{3,2,1,0:T(2,128)S(1)} %copy-done.2, s32[2,2,2]{2,1,0:T(2,128)S(1)} %copy-done.3, bf16[320,2560]{1,0:T(8,128)(2,1)S(1)} %copy-done), custom_call_target="tpu_custom_call" | custom-call | tf_op jit(solution)/shard_map/pallas_call | solution.py:210
  3.9 3.1 %collective-permute-start = (f32[8,320]{1,0:T(8,128)S(1)}, f32[8,320]{1,0:T(8,128)S(1)}, u32[]{:S(2)}, u32[]{:S(2)}) collective-permute-start(f32[8,320]{1,0:T(8,128)S(1)} %get-tuple-element.15), channel_id=1, source_target_pairs={{0,1},{1,0},{2,3},{3,2},{4,5},{5,4},{6,7},{7,6},{8,9},{9,8},{10,11... | collective-permute-start | bytes 30728 | tf_op jit(solution)/shard_map/ppermute | solution.py:33
  7.1 1.7 %collective-permute-done = f32[8,320]{1,0:T(8,128)S(1)} collective-permute-done((f32[8,320]{1,0:T(8,128)S(1)}, f32[8,320]{1,0:T(8,128)S(1)}, u32[]{:S(2)}, u32[]{:S(2)}) %collective-permute-start) | collective-permute-done | bytes 10272 | tf_op jit(solution)/shard_map/ppermute | solution.py:33
  8.8 3.1 %collective-permute-start.2 = (f32[4,320]{1,0:T(4,128)S(1)}, f32[4,320]{1,0:T(4,128)S(1)}, u32[]{:S(2)}, u32[]{:S(2)}) collective-permute-start(f32[4,320]{1,0:T(4,128)S(1)} %get-tuple-element.27), channel_id=1, source_target_pairs={{0,2},{1,3},{2,0},{3,1},{4,20},{5,21},{6,22},{7,23},{8,10},{9,11},... | collective-permute-start | bytes 15368 | tf_op jit(solution)/shard_map/ppermute | solution.py:33
  11.9 1.5 %collective-permute-start.1 = (f32[4,320]{1,0:T(4,128)S(1)}, f32[4,320]{1,0:T(4,128)S(1)}, u32[]{:S(2)}, u32[]{:S(2)}) collective-permute-start(f32[4,320]{1,0:T(4,128)S(1)} %get-tuple-element.28), channel_id=1, source_target_pairs={{0,16},{1,17},{2,18},{3,19},{4,6},{5,7},{6,4},{7,5},{8,24},{9,25},... | collective-permute-start | bytes 15368 | tf_op jit(solution)/shard_map/ppermute | solution.py:33
  13.4 0.1 collective-permute-done.2.second_ref
  13.5 2.0 %collective-permute-done.1.first_ref = f32[4,320]{1,0:T(4,128)S(1)} collective-permute-done((f32[4,320]{1,0:T(4,128)S(1)}, f32[4,320]{1,0:T(4,128)S(1)}, u32[]{:S(2)}, u32[]{:S(2)}) %collective-permute-start.1) | collective-permute-done | bytes 5152 | tf_op jit(solution)/shard_map/ppermute | solution.py:33
  15.5 0.0 copy-start.1
  15.5 1.4 %copy-done.1 = bf16[320,2560]{1,0:T(8,128)(2,1)S(1)} copy-done((bf16[320,2560]{1,0:T(8,128)(2,1)S(1)}, bf16[320,2560]{1,0:T(8,128)(2,1)}, u32[]{:S(2)}) %copy-start.1) | copy-done | bytes 1638424
  16.9 0.3 shard_map.38
  17.3 0.0 collective-permute-start.3
  17.3 1.2 %collective-permute-done.3 = f32[4,2688]{1,0:T(4,128)S(1)} collective-permute-done((f32[4,2688]{1,0:T(4,128)S(1)}, f32[4,2688]{1,0:T(4,128)S(1)}, u32[]{:S(2)}, u32[]{:S(2)}) %collective-permute-start.3) | collective-permute-done | bytes 43040 | tf_op jit(solution)/shard_map/ppermute | solution.py:33
  18.5 1.6 %collective-permute-start.4 = (f32[4,2688]{1,0:T(4,128)S(1)}, f32[4,2688]{1,0:T(4,128)S(1)}, u32[]{:S(2)}, u32[]{:S(2)}) collective-permute-start(f32[4,2688]{1,0:T(4,128)S(1)} %add.25), channel_id=1, source_target_pairs={{0,8},{1,9},{2,10},{3,11},{4,12},{5,13},{6,14},{7,15},{8,0},{9,1},... | collective-permute-start | bytes 129032 | tf_op jit(solution)/shard_map/ppermute | solution.py:33
  20.1 2.5 %collective-permute-done.4 = f32[4,2688]{1,0:T(4,128)S(1)} collective-permute-done((f32[4,2688]{1,0:T(4,128)S(1)}, f32[4,2688]{1,0:T(4,128)S(1)}, u32[]{:S(2)}, u32[]{:S(2)}) %collective-permute-start.4) | collective-permute-done | bytes 43040 | tf_op jit(solution)/shard_map/ppermute | solution.py:33
  22.6 1.6 %collective-permute-start.5 = (f32[4,2688]{1,0:T(4,128)S(1)}, f32[4,2688]{1,0:T(4,128)S(1)}, u32[]{:S(2)}, u32[]{:S(2)}) collective-permute-start(f32[4,2688]{1,0:T(4,128)S(1)} %add.26), channel_id=1, source_target_pairs={{0,16},{1,17},{2,18},{3,19},{4,6},{5,7},{6,4},{7,5},{8,24},{9,25},... | collective-permute-start | bytes 129032 | tf_op jit(solution)/shard_map/ppermute | solution.py:33
  24.2 2.5 %collective-permute-done.5 = f32[4,2688]{1,0:T(4,128)S(1)} collective-permute-done((f32[4,2688]{1,0:T(4,128)S(1)}, f32[4,2688]{1,0:T(4,128)S(1)}, u32[]{:S(2)}, u32[]{:S(2)}) %collective-permute-start.5) | collective-permute-done | bytes 43040 | tf_op jit(solution)/shard_map/ppermute | solution.py:33
  26.7 0.1 collective-permute-start.6
  26.8 1.2 %collective-permute-done.6.other_ref = f32[4,2688]{1,0:T(4,128)S(1)} collective-permute-done((f32[4,2688]{1,0:T(4,128)S(1)}, f32[4,2688]{1,0:T(4,128)S(1)}, u32[]{:S(2)}, u32[]{:S(2)}) %collective-permute-start.6) | collective-permute-done | bytes 43040 | tf_op jit(solution)/shard_map/ppermute | solution.py:33
  28.0 1.0 %shard_map.39 = (f32[8,320]{1,0:T(8,128)S(1)}, f32[8,2560]{1,0:T(8,128)S(1)}) custom-call(f32[4,2688]{1,0:T(4,128)S(1)} %add.27.mine_ref, f32[4,2688]{1,0:T(4,128)S(1)} %collective-permute-done.6.other_ref, f32[8,128]{1,0:T(8,128)S(1)} %get-tuple-element.18.scaling_ref, f32[8,320]{1,0:T(8,128)S(1)} %get-tuple-element.19.left_ref.refs_0_.first_ref, ...), custom_call_target="tpu_custom_call" | custom-call | tf_op jit(solution)/shard_map/pallas_call | solution.py:210
  29.0 1.6 %collective-permute-start.7 = (f32[8,320]{1,0:T(8,128)S(1)}, f32[8,320]{1,0:T(8,128)S(1)}, u32[]{:S(2)}, u32[]{:S(2)}) collective-permute-start(f32[8,320]{1,0:T(8,128)S(1)} %get-tuple-element.20), channel_id=1, source_target_pairs={{0,1},{1,0},{2,3},{3,2},{4,5},{5,4},{6,7},{7,6},{8,9},{9,8},{10,11... | collective-permute-start | bytes 30728 | tf_op jit(solution)/shard_map/ppermute | solution.py:33
  30.6 2.1 %collective-permute-done.7 = f32[8,320]{1,0:T(8,128)S(1)} collective-permute-done((f32[8,320]{1,0:T(8,128)S(1)}, f32[8,320]{1,0:T(8,128)S(1)}, u32[]{:S(2)}, u32[]{:S(2)}) %collective-permute-start.7) | collective-permute-done | bytes 10272 | tf_op jit(solution)/shard_map/ppermute | solution.py:33
  32.8 1.0 %collective-permute-start.9 = (f32[4,320]{1,0:T(4,128)S(1)}, f32[4,320]{1,0:T(4,128)S(1)}, u32[]{:S(2)}, u32[]{:S(2)}) collective-permute-start(f32[4,320]{1,0:T(4,128)S(1)} %get-tuple-element.25), channel_id=1, source_target_pairs={{0,2},{1,3},{2,0},{3,1},{4,20},{5,21},{6,22},{7,23},{8,10},{9,11},... | collective-permute-start | bytes 15368 | tf_op jit(solution)/shard_map/ppermute | solution.py:33
  33.7 1.5 %collective-permute-start.8 = (f32[4,320]{1,0:T(4,128)S(1)}, f32[4,320]{1,0:T(4,128)S(1)}, u32[]{:S(2)}, u32[]{:S(2)}) collective-permute-start(f32[4,320]{1,0:T(4,128)S(1)} %get-tuple-element.26), channel_id=1, source_target_pairs={{0,16},{1,17},{2,18},{3,19},{4,6},{5,7},{6,4},{7,5},{8,24},{9,25},... | collective-permute-start | bytes 15368 | tf_op jit(solution)/shard_map/ppermute | solution.py:33
  35.2 2.1 %collective-permute-done.9.second_ref = f32[4,320]{1,0:T(4,128)S(1)} collective-permute-done((f32[4,320]{1,0:T(4,128)S(1)}, f32[4,320]{1,0:T(4,128)S(1)}, u32[]{:S(2)}, u32[]{:S(2)}) %collective-permute-start.9) | collective-permute-done | bytes 5152 | tf_op jit(solution)/shard_map/ppermute | solution.py:33
  37.4 0.0 collective-permute-done.8.first_ref
  37.4 0.6 %shard_map.40 = (f32[8,320]{1,0:T(8,128)S(1)}, f32[4,2688]{1,0:T(4,128)S(1)}, f32[4,2688]{1,0:T(4,128)S(1)}) custom-call(f32[8,320]{1,0:T(8,128)S(1)} %add.28.images_ref, f32[4,320]{1,0:T(4,128)S(1)} %collective-permute-done.8.first_ref, f32[4,320]{1,0:T(4,128)S(1)} %collective-permute-done.9.second_ref, bf16[320,2560]{1,0:T(8,128)(2,1)S(1)} %copy-done.1, ...), custom_call_target="tpu_custom_call" | custom-call | tf_op jit(solution)/shard_map/pallas_call | solution.py:210
  37.9 0.1 collective-permute-start.10
  38.0 1.2 %collective-permute-done.10 = f32[4,2688]{1,0:T(4,128)S(1)} collective-permute-done((f32[4,2688]{1,0:T(4,128)S(1)}, f32[4,2688]{1,0:T(4,128)S(1)}, u32[]{:S(2)}, u32[]{:S(2)}) %collective-permute-start.10) | collective-permute-done | bytes 43040 | tf_op jit(solution)/shard_map/ppermute | solution.py:33
  39.2 1.6 %collective-permute-start.11 = (f32[4,2688]{1,0:T(4,128)S(1)}, f32[4,2688]{1,0:T(4,128)S(1)}, u32[]{:S(2)}, u32[]{:S(2)}) collective-permute-start(f32[4,2688]{1,0:T(4,128)S(1)} %add.29), channel_id=1, source_target_pairs={{0,8},{1,9},{2,10},{3,11},{4,12},{5,13},{6,14},{7,15},{8,0},{9,1},... | collective-permute-start | bytes 129032 | tf_op jit(solution)/shard_map/ppermute | solution.py:33
  40.8 2.5 %collective-permute-done.11 = f32[4,2688]{1,0:T(4,128)S(1)} collective-permute-done((f32[4,2688]{1,0:T(4,128)S(1)}, f32[4,2688]{1,0:T(4,128)S(1)}, u32[]{:S(2)}, u32[]{:S(2)}) %collective-permute-start.11) | collective-permute-done | bytes 43040 | tf_op jit(solution)/shard_map/ppermute | solution.py:33
  43.3 1.6 %collective-permute-start.12 = (f32[4,2688]{1,0:T(4,128)S(1)}, f32[4,2688]{1,0:T(4,128)S(1)}, u32[]{:S(2)}, u32[]{:S(2)}) collective-permute-start(f32[4,2688]{1,0:T(4,128)S(1)} %add.30), channel_id=1, source_target_pairs={{0,16},{1,17},{2,18},{3,19},{4,6},{5,7},{6,4},{7,5},{8,24},{9,25},... | collective-permute-start | bytes 129032 | tf_op jit(solution)/shard_map/ppermute | solution.py:33
  44.9 2.5 %collective-permute-done.12 = f32[4,2688]{1,0:T(4,128)S(1)} collective-permute-done((f32[4,2688]{1,0:T(4,128)S(1)}, f32[4,2688]{1,0:T(4,128)S(1)}, u32[]{:S(2)}, u32[]{:S(2)}) %collective-permute-start.12) | collective-permute-done | bytes 43040 | tf_op jit(solution)/shard_map/ppermute | solution.py:33
  47.4 0.1 collective-permute-start.13
  47.5 1.2 %collective-permute-done.13.other_ref = f32[4,2688]{1,0:T(4,128)S(1)} collective-permute-done((f32[4,2688]{1,0:T(4,128)S(1)}, f32[4,2688]{1,0:T(4,128)S(1)}, u32[]{:S(2)}, u32[]{:S(2)}) %collective-permute-start.13) | collective-permute-done | bytes 43040 | tf_op jit(solution)/shard_map/ppermute | solution.py:33
  48.7 2.3 %shard_map.41 = f32[320,2560]{1,0:T(8,128)} custom-call(f32[4,2688]{1,0:T(4,128)S(1)} %add.31.mine_ref, f32[4,2688]{1,0:T(4,128)S(1)} %collective-permute-done.13.other_ref, f32[8,128]{1,0:T(8,128)S(1)} %get-tuple-element.18.scaling_ref, f32[8,320]{1,0:T(8,128)S(1)} %get-tuple-element.19.left_ref.refs_0_.first_ref, ...), custom_call_target="tpu_custom_call" | custom-call | tf_op jit(solution)/shard_map/pallas_call | solution.py:210
  (10 shorter events, 0.1 us)
Async XLA Ops:
  0.0 1.4 %copy-start = (bf16[320,2560]{1,0:T(8,128)(2,1)S(1)}, bf16[320,2560]{1,0:T(8,128)(2,1)}, u32[]{:S(2)}) copy-start(bf16[320,2560]{1,0:T(8,128)(2,1)} %replicas_ref.7) | copy-start | bytes 4915204
  1.4 0.7 %copy-start.2 = (s32[2,2,2,2]{3,2,1,0:T(2,128)S(1)}, s32[2,2,2,2]{3,2,1,0:T(2,128)}, u32[]{:S(2)}) copy-start(s32[2,2,2,2]{3,2,1,0:T(2,128)} %seeds_ref.1) | copy-start | bytes 196
  2.1 0.7 %copy-start.3 = (s32[2,2,2]{2,1,0:T(2,128)S(1)}, s32[2,2,2]{2,1,0:T(2,128)}, u32[]{:S(2)}) copy-start(s32[2,2,2]{2,1,0:T(2,128)} %counts_ref.1) | copy-start | bytes 100
  3.9 4.8 %collective-permute-start = (f32[8,320]{1,0:T(8,128)S(1)}, f32[8,320]{1,0:T(8,128)S(1)}, u32[]{:S(2)}, u32[]{:S(2)}) collective-permute-start(f32[8,320]{1,0:T(8,128)S(1)} %get-tuple-element.15), channel_id=1, source_target_pairs={{0,1},{1,0},{2,3},{3,2},{4,5},{5,4},{6,7},{7,6},{8,9},{9,8},{10,11... | collective-permute-start | bytes 30728 | tf_op jit(solution)/shard_map/ppermute | solution.py:33
  8.8 4.7 %collective-permute-start.2 = (f32[4,320]{1,0:T(4,128)S(1)}, f32[4,320]{1,0:T(4,128)S(1)}, u32[]{:S(2)}, u32[]{:S(2)}) collective-permute-start(f32[4,320]{1,0:T(4,128)S(1)} %get-tuple-element.27), channel_id=1, source_target_pairs={{0,2},{1,3},{2,0},{3,1},{4,20},{5,21},{6,22},{7,23},{8,10},{9,11},... | collective-permute-start | bytes 15368 | tf_op jit(solution)/shard_map/ppermute | solution.py:33
  11.9 3.6 %collective-permute-start.1 = (f32[4,320]{1,0:T(4,128)S(1)}, f32[4,320]{1,0:T(4,128)S(1)}, u32[]{:S(2)}, u32[]{:S(2)}) collective-permute-start(f32[4,320]{1,0:T(4,128)S(1)} %get-tuple-element.28), channel_id=1, source_target_pairs={{0,16},{1,17},{2,18},{3,19},{4,6},{5,7},{6,4},{7,5},{8,24},{9,25},... | collective-permute-start | bytes 15368 | tf_op jit(solution)/shard_map/ppermute | solution.py:33
  15.5 1.4 %copy-start.1 = (bf16[320,2560]{1,0:T(8,128)(2,1)S(1)}, bf16[320,2560]{1,0:T(8,128)(2,1)}, u32[]{:S(2)}) copy-start(bf16[320,2560]{1,0:T(8,128)(2,1)} %replicas_ref.7) | copy-start | bytes 4915204
  17.3 1.3 %collective-permute-start.3 = (f32[4,2688]{1,0:T(4,128)S(1)}, f32[4,2688]{1,0:T(4,128)S(1)}, u32[]{:S(2)}, u32[]{:S(2)}) collective-permute-start(f32[4,2688]{1,0:T(4,128)S(1)} %get-tuple-element.17), channel_id=1, source_target_pairs={{0,4},{1,5},{2,6},{3,7},{4,0},{5,1},{6,2},{7,3},{8,12},{9,13},{10,... | collective-permute-start | bytes 129032 | tf_op jit(solution)/shard_map/ppermute | solution.py:33
  18.5 4.1 %collective-permute-start.4 = (f32[4,2688]{1,0:T(4,128)S(1)}, f32[4,2688]{1,0:T(4,128)S(1)}, u32[]{:S(2)}, u32[]{:S(2)}) collective-permute-start(f32[4,2688]{1,0:T(4,128)S(1)} %add.25), channel_id=1, source_target_pairs={{0,8},{1,9},{2,10},{3,11},{4,12},{5,13},{6,14},{7,15},{8,0},{9,1},... | collective-permute-start | bytes 129032 | tf_op jit(solution)/shard_map/ppermute | solution.py:33
  22.6 4.1 %collective-permute-start.5 = (f32[4,2688]{1,0:T(4,128)S(1)}, f32[4,2688]{1,0:T(4,128)S(1)}, u32[]{:S(2)}, u32[]{:S(2)}) collective-permute-start(f32[4,2688]{1,0:T(4,128)S(1)} %add.26), channel_id=1, source_target_pairs={{0,16},{1,17},{2,18},{3,19},{4,6},{5,7},{6,4},{7,5},{8,24},{9,25},... | collective-permute-start | bytes 129032 | tf_op jit(solution)/shard_map/ppermute | solution.py:33
  26.7 1.3 %collective-permute-start.6 = (f32[4,2688]{1,0:T(4,128)S(1)}, f32[4,2688]{1,0:T(4,128)S(1)}, u32[]{:S(2)}, u32[]{:S(2)}) collective-permute-start(f32[4,2688]{1,0:T(4,128)S(1)} %add.27.mine_ref), channel_id=1, source_target_pairs={{0,4},{1,5},{2,6},{3,7},{4,0},{5,1},{6,2},{7,3},{8,12},{9,13},{10,... | collective-permute-start | bytes 129032 | tf_op jit(solution)/shard_map/ppermute | solution.py:33
  29.0 3.7 %collective-permute-start.7 = (f32[8,320]{1,0:T(8,128)S(1)}, f32[8,320]{1,0:T(8,128)S(1)}, u32[]{:S(2)}, u32[]{:S(2)}) collective-permute-start(f32[8,320]{1,0:T(8,128)S(1)} %get-tuple-element.20), channel_id=1, source_target_pairs={{0,1},{1,0},{2,3},{3,2},{4,5},{5,4},{6,7},{7,6},{8,9},{9,8},{10,11... | collective-permute-start | bytes 30728 | tf_op jit(solution)/shard_map/ppermute | solution.py:33
  32.8 4.6 %collective-permute-start.9 = (f32[4,320]{1,0:T(4,128)S(1)}, f32[4,320]{1,0:T(4,128)S(1)}, u32[]{:S(2)}, u32[]{:S(2)}) collective-permute-start(f32[4,320]{1,0:T(4,128)S(1)} %get-tuple-element.25), channel_id=1, source_target_pairs={{0,2},{1,3},{2,0},{3,1},{4,20},{5,21},{6,22},{7,23},{8,10},{9,11},... | collective-permute-start | bytes 15368 | tf_op jit(solution)/shard_map/ppermute | solution.py:33
  33.7 3.6 %collective-permute-start.8 = (f32[4,320]{1,0:T(4,128)S(1)}, f32[4,320]{1,0:T(4,128)S(1)}, u32[]{:S(2)}, u32[]{:S(2)}) collective-permute-start(f32[4,320]{1,0:T(4,128)S(1)} %get-tuple-element.26), channel_id=1, source_target_pairs={{0,16},{1,17},{2,18},{3,19},{4,6},{5,7},{6,4},{7,5},{8,24},{9,25},... | collective-permute-start | bytes 15368 | tf_op jit(solution)/shard_map/ppermute | solution.py:33
  37.9 1.3 %collective-permute-start.10 = (f32[4,2688]{1,0:T(4,128)S(1)}, f32[4,2688]{1,0:T(4,128)S(1)}, u32[]{:S(2)}, u32[]{:S(2)}) collective-permute-start(f32[4,2688]{1,0:T(4,128)S(1)} %get-tuple-element.23), channel_id=1, source_target_pairs={{0,4},{1,5},{2,6},{3,7},{4,0},{5,1},{6,2},{7,3},{8,12},{9,13},{10,... | collective-permute-start | bytes 129032 | tf_op jit(solution)/shard_map/ppermute | solution.py:33
  39.2 4.1 %collective-permute-start.11 = (f32[4,2688]{1,0:T(4,128)S(1)}, f32[4,2688]{1,0:T(4,128)S(1)}, u32[]{:S(2)}, u32[]{:S(2)}) collective-permute-start(f32[4,2688]{1,0:T(4,128)S(1)} %add.29), channel_id=1, source_target_pairs={{0,8},{1,9},{2,10},{3,11},{4,12},{5,13},{6,14},{7,15},{8,0},{9,1},... | collective-permute-start | bytes 129032 | tf_op jit(solution)/shard_map/ppermute | solution.py:33
  43.3 4.1 %collective-permute-start.12 = (f32[4,2688]{1,0:T(4,128)S(1)}, f32[4,2688]{1,0:T(4,128)S(1)}, u32[]{:S(2)}, u32[]{:S(2)}) collective-permute-start(f32[4,2688]{1,0:T(4,128)S(1)} %add.30), channel_id=1, source_target_pairs={{0,16},{1,17},{2,18},{3,19},{4,6},{5,7},{6,4},{7,5},{8,24},{9,25},... | collective-permute-start | bytes 129032 | tf_op jit(solution)/shard_map/ppermute | solution.py:33
  47.4 1.3 %collective-permute-start.13 = (f32[4,2688]{1,0:T(4,128)S(1)}, f32[4,2688]{1,0:T(4,128)S(1)}, u32[]{:S(2)}, u32[]{:S(2)}) collective-permute-start(f32[4,2688]{1,0:T(4,128)S(1)} %add.31.mine_ref), channel_id=1, source_target_pairs={{0,4},{1,5},{2,6},{3,7},{4,0},{5,1},{6,2},{7,3},{8,12},{9,13},{10,... | collective-permute-start | bytes 129032 | tf_op jit(solution)/shard_map/ppermute | solution.py:33

commit v3 on v2

--- a/solution.py
+++ b/solution.py
@@ -109,24 +109,45 @@
     return values
 
 
-def first_kernel(layout, seeds_ref, counts_ref, replicas_ref, images_ref, scaling_ref):
+def first_kernel(
+    layout, seeds_hbm, counts_hbm, replicas_hbm, images_ref, scaling_ref, replicas_ref, seeds_ref, counts_ref, sems
+):
+    size = replicas_ref.shape[1] // CHUNKS
+    blocks = [pl.ds(k * size, size) for k in range(CHUNKS)]
+    small = [
+        pltpu.make_async_copy(seeds_hbm, seeds_ref, sems.at[CHUNKS]),
+        pltpu.make_async_copy(counts_hbm, counts_ref, sems.at[CHUNKS + 1]),
+    ]
+    copies = [
+        pltpu.make_async_copy(replicas_hbm.at[:, block], replicas_ref.at[:, block], sems.at[k])
+        for k, block in enumerate(blocks)
+    ]
+    for copy in small + copies:
+        copy.start()
+    column = layout.first_column(replicas_ref.shape[1]) + lax.broadcasted_iota(
+        jnp.int32, (8, replicas_ref.shape[1]), 1
+    )
+    square = remainder(column * column)
     edges = layout.edges()
+    for copy in small:
+        copy.wait()
     seeds = row_values([seeds_ref[r, c, a, k] for r, c, a in edges for k in range(2)], LANES)
     counts = row_values([counts_ref[r, c, a] for r, c, a in edges for k in range(2)], LANES)
     scaling_ref[...] = -(counts.astype(jnp.float32) / 16.0)
-    width = replicas_ref.shape[1]
-    column = layout.first_column(width) + lax.broadcasted_iota(jnp.int32, (8, width), 1)
-    square = remainder(column * column)
     residue = remainder(square * (seeds[:, :1] + 1) + column * 17)
-    factors = residue.astype(jnp.float32) * (2.0 / MODULUS) - 1.0
-    images_ref[...] = folded(dot(stacked(factors), replicas_ref[...], over_last))
+    factors = stacked(residue.astype(jnp.float32) * (2.0 / MODULUS) - 1.0)
+    images = 0.0
+    for k, block in enumerate(blocks):
+        copies[k].wait()
+        images = images + dot(factors[:, k * size : (k + 1) * size], replicas_ref[:, block], over_last)
+    images_ref[...] = folded(images)
 
 
 def project_kernel(has_update, images_ref, first_ref, second_ref, replicas_ref, *refs):
     if has_update:
-        earlier_ref, right_ref, left_ref, keep_ref, send_ref = refs
+        earlier_ref, right_ref, left_ref, packed_ref = refs
     else:
-        left_ref, keep_ref, send_ref = refs
+        left_ref, packed_ref = refs
     left_ref[0:4] = images_ref[0:4] - first_ref[...]
     left_ref[4:8] = images_ref[4:8] - second_ref[...]
     left = left_ref[...]
@@ -140,18 +161,11 @@
     norm = jnp.sum(left * left, 1, keepdims=True)
     inner = jnp.sum(left * partner, 1, keepdims=True)
     lanes = lax.broadcasted_iota(jnp.int32, (8, LANES), 1)
-    tail = jnp.where(lanes == 0, norm, inner)
-    keep_ref[:, :width] = projections[0:4]
-    send_ref[:, :width] = projections[4:8]
-    keep_ref[:, width:] = tail[0:4]
-    send_ref[:, width:] = tail[4:8]
-
-
-def orthonormal_factors(mine_ref, other_ref, scaling, total_ref):
-    total_ref[0:4] = mine_ref[...]
-    total_ref[4:8] = other_ref[...]
-    width = total_ref.shape[1] - LANES
-    raw = total_ref[:, :width]
+    packed_ref[:, :width] = projections
+    packed_ref[:, width:] = jnp.where(lanes == 0, norm, inner)
+
+
+def coefficients(total_ref, width):
     tail = 0.5 * total_ref[:, width:]
     even = lax.broadcasted_iota(jnp.int32, (8, LANES), 0) % 2 == 0
     after, before = pltpu.roll(tail, 7, 0), pltpu.roll(tail, 1, 0)
@@ -166,13 +180,21 @@
     mixed = -correlation / (lead_root * rest_root)
     even = even[:, 0:1]
     own = jnp.where(even, 1.0 / lead_root, 1.0 / rest_root)
-    factors = own * raw + jnp.where(even, 0.0, mixed) * pltpu.roll(raw, 1, 0)
-    right = own * factors + jnp.where(even, mixed, 0.0) * pltpu.roll(factors, 7, 0)
-    return factors, scaling * right
+    return own, jnp.where(even, 0.0, mixed), jnp.where(even, mixed, 0.0)
+
+
+def right_factors(raw, scaling, own, from_before, from_after):
+    factors = own * raw + from_before * pltpu.roll(raw, 1, 0)
+    return factors, scaling * (own * factors + from_after * pltpu.roll(factors, 7, 0))
 
 
 def images_kernel(mine_ref, other_ref, scaling_ref, left_ref, replicas_ref, images_ref, right_ref, total_ref):
-    factors, right = orthonormal_factors(mine_ref, other_ref, scaling_ref[:, 0:1], total_ref)
+    total_ref[0:4] = mine_ref[...]
+    total_ref[4:8] = other_ref[...]
+    width = replicas_ref.shape[1]
+    factors, right = right_factors(
+        total_ref[:, :width], scaling_ref[:, 0:1], *coefficients(total_ref, width)
+    )
     right_ref[...] = right
     images = folded(dot(stacked(factors), replicas_ref[...], over_last))
     cross = full_product(factors, right, over_last)
@@ -180,22 +202,24 @@
 
 
 def update_kernel(
-    mine_ref, other_ref, scaling_ref, first_ref, second_ref, right_ref, out_ref, total_ref, terms_ref, block_ref, sems
+    mine_ref, other_ref, scaling_ref, first_ref, second_ref, right_ref, out_ref, total_ref, block_ref, sems
 ):
-    _, right = orthonormal_factors(mine_ref, other_ref, scaling_ref[:, 0:1], total_ref)
+    total_ref[0:4] = mine_ref[...]
+    total_ref[4:8] = other_ref[...]
+    parts = coefficients(total_ref, right_ref.shape[1])
+    scaling = scaling_ref[:, 0:1]
     lefts = jnp.concatenate([first_ref[...], second_ref[...]], 0)
     left_high = lefts.astype(jnp.bfloat16).astype(jnp.float32)
     left_terms = jnp.concatenate([left_high, lefts - left_high, left_high], 0).astype(jnp.bfloat16)
-    rights = jnp.concatenate([right_ref[...], right], 0)
-    right_high = rights.astype(jnp.bfloat16).astype(jnp.float32)
-    terms_ref[...] = jnp.concatenate([right_high, right_high, rights - right_high], 0).astype(
-        jnp.bfloat16
-    )
     size = block_ref.shape[2]
     copies = []
     for k in range(block_ref.shape[0]):
         columns = pl.ds(k * size, size)
-        block_ref[k] = dot(left_terms, terms_ref[:, columns], over_first)
+        _, right = right_factors(total_ref[:, columns], scaling, *parts)
+        rights = jnp.concatenate([right_ref[:, columns], right], 0)
+        right_high = rights.astype(jnp.bfloat16).astype(jnp.float32)
+        right_terms = jnp.concatenate([right_high, right_high, rights - right_high], 0)
+        block_ref[k] = dot(left_terms, right_terms.astype(jnp.bfloat16), over_first)
         copies.append(pltpu.make_async_copy(block_ref.at[k], out_ref.at[:, columns], sems.at[k]))
         copies[-1].start()
     for copy in copies:
@@ -203,13 +227,13 @@
 
 
 vmem = pl.BlockSpec(memory_space=pltpu.VMEM)
-smem = pl.BlockSpec(memory_space=pltpu.SMEM)
+hbm = pl.BlockSpec(memory_space=pltpu.HBM)
 
 
 def call(kernel, outs, *args, in_specs=None, out_specs=None, scratch=()):
     return pl.pallas_call(
         kernel,
-        out_shape=[jax.ShapeDtypeStruct(shape, jnp.float32) for shape in outs],
+        out_shape=outs,
         in_specs=in_specs or [vmem] * len(args),
         out_specs=out_specs or [vmem] * len(outs),
         scratch_shapes=list(scratch),
@@ -217,8 +241,12 @@
     )(*args)
 
 
-def per_device(replicas, factor_seeds, edge_counts):
-    height, width = replicas.shape
+def single(*shape):
+    return jax.ShapeDtypeStruct(shape, jnp.float32)
+
+
+def per_device(replicas_hbm, factor_seeds, edge_counts):
+    height, width = replicas_hbm.shape
     packed = width + LANES
     layout = Layout(*factor_seeds.shape[:2])
     total_scratch = pltpu.VMEM((8, packed), jnp.float32)
@@ -228,60 +256,61 @@
             images = images + layout.col_swap(images, bit)
         return images, layout.neighbours(images[:4], 0), layout.neighbours(images[4:], 1)
 
-    def summed(keep, send):
-        total = keep + layout.row_swap(send, 0)
-        for bit in range(1, layout.shards[0].bit_length() - 1):
+    def summed(values):
+        other = layout.row_swap(values, 0)
+        total, rest = values[:4] + other[4:], values[4:] + other[:4]
+        if layout.shards[0] > 2:
+            total = total + layout.exchange(rest, lambda r, c: (r ^ 3, c))
+        for bit in range(2, layout.shards[0].bit_length() - 1):
             total = total + layout.row_swap(total, bit)
         total = total + layout.neighbours(total, 0)
         return total, layout.row_swap(total, 0)
 
-    images, scaling = call(
+    images, scaling, replicas = call(
         functools.partial(first_kernel, layout),
-        [(8, height), (8, LANES)],
-        factor_seeds,
-        edge_counts,
-        replicas,
-        in_specs=[smem, smem, vmem],
-    )
-    left_one, keep, send = call(
+        [single(8, height), single(8, LANES), jax.ShapeDtypeStruct((height, width), replicas_hbm.dtype)],
+        *(pltpu.with_memory_space_constraint(array, pltpu.HBM) for array in (factor_seeds, edge_counts, replicas_hbm)),
+        in_specs=[hbm] * 3,
+        scratch=[
+            pltpu.SMEM(factor_seeds.shape, jnp.int32),
+            pltpu.SMEM(edge_counts.shape, jnp.int32),
+            pltpu.SemaphoreType.DMA((CHUNKS + 2,)),
+        ],
+    )
+    left_one, values = call(
         functools.partial(project_kernel, False),
-        [(8, height), (4, packed), (4, packed)],
+        [single(8, height), single(8, packed)],
         *reduced(images),
         replicas,
     )
-    mine, other = summed(keep, send)
     images, right_one = call(
         images_kernel,
-        [(8, height), (8, width)],
-        mine,
-        other,
+        [single(8, height), single(8, width)],
+        *summed(values),
         scaling,
         left_one,
         replicas,
         scratch=[total_scratch],
     )
-    left_two, keep, send = call(
+    left_two, values = call(
         functools.partial(project_kernel, True),
-        [(8, height), (4, packed), (4, packed)],
+        [single(8, height), single(8, packed)],
         *reduced(images),
         replicas,
         left_one,
         right_one,
     )
-    mine, other = summed(keep, send)
     (update,) = call(
         update_kernel,
-        [(height, width)],
-        mine,
-        other,
+        [single(height, width)],
+        *summed(values),
         scaling,
         left_one,
         left_two,
         right_one,
-        out_specs=[pl.BlockSpec(memory_space=pl.ANY)],
+        out_specs=[hbm],
         scratch=[
             total_scratch,
-            pltpu.VMEM((48, width), jnp.bfloat16),
             pltpu.VMEM((CHUNKS, height, width // CHUNKS), jnp.float32),
             pltpu.SemaphoreType.DMA((CHUNKS,)),
         ],

time: 51.2 us -> 47.1 us (0.920)
  local copies, waits for them, and re-layouts: 4.24 us -> 0.01 us
  Pallas kernels: 5.32 us -> 6.24 us
  starting transfers between devices: 18.4 us -> 17.8 us
    unnamed x8 -> x0, local copies, waits for them, and re-layouts: 4.23 us -> none
    pallas_call x5, Pallas kernels: 5.32 us -> 6.24 us  [call(): pl.pallas_call(kernel, out_shape=outs, in_specs=in_specs or [vmem] * len(...]
    ppermute x14, starting transfers between devices: 18.4 us -> 17.8 us  [exchange(): return lax.ppermute(value, ('row', 'col'), pairs)]
where the time goes in v3:
time: 47.1 us; the launch traced here: 46.9 us
  waiting for transfers between devices  22.6 us (48%)
  starting transfers between devices  17.8 us (38%)
  Pallas kernels  6.24 us (13%)
    ppermute x14, waiting for transfers between devices, exchange(): return lax.ppermute(value, ('row', 'col'), pairs)  22.6 us
    ppermute x14, starting transfers between devices, exchange(): return lax.ppermute(value, ('row', 'col'), pairs)  17.8 us
    pallas_call x5, Pallas kernels, call(): pl.pallas_call(kernel, out_shape=outs, in_specs=in_specs or [vmem] * len(...  6.24 us
  transfers between devices with their start and end apart: 14, of which 13 were waited for; matrix products, arithmetic and copies ran while one was open for 0% of the time, Pallas kernels for 0%

profile of v3, /device:TPU:0, one launch (start us, length us, event | category | flops | bytes accessed | tf_op | source)
XLA Modules:
  0.0 46.9 jit_solution(12748754949972206310)
XLA Ops:
  0.0 2.1 %shard_map.37 = (f32[8,320]{1,0:T(8,128)S(1)}, f32[8,128]{1,0:T(8,128)S(1)}, bf16[320,2560]{1,0:T(8,128)(2,1)S(1)}) custom-call(s32[2,2,2,2]{3,2,1,0:T(2,128)} %seeds_hbm.1, s32[2,2,2]{2,1,0:T(2,128)} %counts_hbm.1, bf16[320,2560]{1,0:T(8,128)(2,1)} %replicas_hbm.1), custom_call_target="tpu_custom_call" | custom-call | tf_op jit(solution)/shard_map/pallas_call | solution.py:234
  2.1 3.1 %collective-permute-start = (f32[8,320]{1,0:T(8,128)S(1)}, f32[8,320]{1,0:T(8,128)S(1)}, u32[]{:S(2)}, u32[]{:S(2)}) collective-permute-start(f32[8,320]{1,0:T(8,128)S(1)} %get-tuple-element.14), channel_id=1, source_target_pairs={{0,1},{1,0},{2,3},{3,2},{4,5},{5,4},{6,7},{7,6},{8,9},{9,8},{10,11... | collective-permute-start | bytes 30728 | tf_op jit(solution)/shard_map/ppermute | solution.py:33
  5.2 1.7 %collective-permute-done = f32[8,320]{1,0:T(8,128)S(1)} collective-permute-done((f32[8,320]{1,0:T(8,128)S(1)}, f32[8,320]{1,0:T(8,128)S(1)}, u32[]{:S(2)}, u32[]{:S(2)}) %collective-permute-start) | collective-permute-done | bytes 10272 | tf_op jit(solution)/shard_map/ppermute | solution.py:33
  6.9 3.1 %collective-permute-start.2 = (f32[4,320]{1,0:T(4,128)S(1)}, f32[4,320]{1,0:T(4,128)S(1)}, u32[]{:S(2)}, u32[]{:S(2)}) collective-permute-start(f32[4,320]{1,0:T(4,128)S(1)} %get-tuple-element.25), channel_id=1, source_target_pairs={{0,2},{1,3},{2,0},{3,1},{4,20},{5,21},{6,22},{7,23},{8,10},{9,11},... | collective-permute-start | bytes 15368 | tf_op jit(solution)/shard_map/ppermute | solution.py:33
  10.0 1.5 %collective-permute-start.1 = (f32[4,320]{1,0:T(4,128)S(1)}, f32[4,320]{1,0:T(4,128)S(1)}, u32[]{:S(2)}, u32[]{:S(2)}) collective-permute-start(f32[4,320]{1,0:T(4,128)S(1)} %get-tuple-element.26), channel_id=1, source_target_pairs={{0,16},{1,17},{2,18},{3,19},{4,6},{5,7},{6,4},{7,5},{8,24},{9,25},... | collective-permute-start | bytes 15368 | tf_op jit(solution)/shard_map/ppermute | solution.py:33
  11.5 0.1 collective-permute-done.2.second_ref
  11.6 2.0 %collective-permute-done.1.first_ref = f32[4,320]{1,0:T(4,128)S(1)} collective-permute-done((f32[4,320]{1,0:T(4,128)S(1)}, f32[4,320]{1,0:T(4,128)S(1)}, u32[]{:S(2)}, u32[]{:S(2)}) %collective-permute-start.1) | collective-permute-done | bytes 5152 | tf_op jit(solution)/shard_map/ppermute | solution.py:33
  13.6 0.3 shard_map.38
  14.0 0.0 collective-permute-start.3
  14.0 1.3 %collective-permute-done.3 = f32[8,2688]{1,0:T(8,128)S(1)} collective-permute-done((f32[8,2688]{1,0:T(8,128)S(1)}, f32[8,2688]{1,0:T(8,128)S(1)}, u32[]{:S(2)}, u32[]{:S(2)}) %collective-permute-start.3) | collective-permute-done | bytes 86048 | tf_op jit(solution)/shard_map/ppermute | solution.py:33
  15.3 1.3 %collective-permute-start.4 = (f32[4,2688]{1,0:T(4,128)S(1)}, f32[4,2688]{1,0:T(4,128)S(1)}, u32[]{:S(2)}, u32[]{:S(2)}) collective-permute-start(f32[4,2688]{1,0:T(4,128)S(1)} %slice_add_fusion.2), channel_id=1, source_target_pairs={{0,12},{1,13},{2,14},{3,15},{4,8},{5,9},{6,10},{7,11},{8,4},{9,5},... | collective-permute-start | bytes 129032 | tf_op jit(solution)/shard_map/ppermute | solution.py:33
  16.6 2.3 %collective-permute-done.4 = f32[4,2688]{1,0:T(4,128)S(1)} collective-permute-done((f32[4,2688]{1,0:T(4,128)S(1)}, f32[4,2688]{1,0:T(4,128)S(1)}, u32[]{:S(2)}, u32[]{:S(2)}) %collective-permute-start.4) | collective-permute-done | bytes 43040 | tf_op jit(solution)/shard_map/ppermute | solution.py:33
  18.9 1.6 %collective-permute-start.5 = (f32[4,2688]{1,0:T(4,128)S(1)}, f32[4,2688]{1,0:T(4,128)S(1)}, u32[]{:S(2)}, u32[]{:S(2)}) collective-permute-start(f32[4,2688]{1,0:T(4,128)S(1)} %fusion.1), channel_id=1, source_target_pairs={{0,16},{1,17},{2,18},{3,19},{4,6},{5,7},{6,4},{7,5},{8,24},{9,25},... | collective-permute-start | bytes 129032 | tf_op jit(solution)/shard_map/ppermute | solution.py:33
  20.5 2.5 %collective-permute-done.5 = f32[4,2688]{1,0:T(4,128)S(1)} collective-permute-done((f32[4,2688]{1,0:T(4,128)S(1)}, f32[4,2688]{1,0:T(4,128)S(1)}, u32[]{:S(2)}, u32[]{:S(2)}) %collective-permute-start.5) | collective-permute-done | bytes 43040 | tf_op jit(solution)/shard_map/ppermute | solution.py:33
  23.0 0.1 collective-permute-start.6
  23.1 1.2 %collective-permute-done.6.other_ref = f32[4,2688]{1,0:T(4,128)S(1)} collective-permute-done((f32[4,2688]{1,0:T(4,128)S(1)}, f32[4,2688]{1,0:T(4,128)S(1)}, u32[]{:S(2)}, u32[]{:S(2)}) %collective-permute-start.6) | collective-permute-done | bytes 43040 | tf_op jit(solution)/shard_map/ppermute | solution.py:33
  24.3 1.0 %shard_map.39 = (f32[8,320]{1,0:T(8,128)S(1)}, f32[8,2560]{1,0:T(8,128)S(1)}) custom-call(f32[4,2688]{1,0:T(4,128)S(1)} %add.34.mine_ref, f32[4,2688]{1,0:T(4,128)S(1)} %collective-permute-done.6.other_ref, f32[8,128]{1,0:T(8,128)S(1)} %get-tuple-element.17.scaling_ref, f32[8,320]{1,0:T(8,128)S(1)} %get-tuple-element.18.left_ref.refs_0_.first_ref, ...), custom_call_target="tpu_custom_call" | custom-call | tf_op jit(solution)/shard_map/pallas_call | solution.py:234
  25.3 1.6 %collective-permute-start.7 = (f32[8,320]{1,0:T(8,128)S(1)}, f32[8,320]{1,0:T(8,128)S(1)}, u32[]{:S(2)}, u32[]{:S(2)}) collective-permute-start(f32[8,320]{1,0:T(8,128)S(1)} %get-tuple-element.19), channel_id=1, source_target_pairs={{0,1},{1,0},{2,3},{3,2},{4,5},{5,4},{6,7},{7,6},{8,9},{9,8},{10,11... | collective-permute-start | bytes 30728 | tf_op jit(solution)/shard_map/ppermute | solution.py:33
  26.9 2.1 %collective-permute-done.7 = f32[8,320]{1,0:T(8,128)S(1)} collective-permute-done((f32[8,320]{1,0:T(8,128)S(1)}, f32[8,320]{1,0:T(8,128)S(1)}, u32[]{:S(2)}, u32[]{:S(2)}) %collective-permute-start.7) | collective-permute-done | bytes 10272 | tf_op jit(solution)/shard_map/ppermute | solution.py:33
  29.1 1.0 %collective-permute-start.9 = (f32[4,320]{1,0:T(4,128)S(1)}, f32[4,320]{1,0:T(4,128)S(1)}, u32[]{:S(2)}, u32[]{:S(2)}) collective-permute-start(f32[4,320]{1,0:T(4,128)S(1)} %get-tuple-element.23), channel_id=1, source_target_pairs={{0,2},{1,3},{2,0},{3,1},{4,20},{5,21},{6,22},{7,23},{8,10},{9,11},... | collective-permute-start | bytes 15368 | tf_op jit(solution)/shard_map/ppermute | solution.py:33
  30.0 1.5 %collective-permute-start.8 = (f32[4,320]{1,0:T(4,128)S(1)}, f32[4,320]{1,0:T(4,128)S(1)}, u32[]{:S(2)}, u32[]{:S(2)}) collective-permute-start(f32[4,320]{1,0:T(4,128)S(1)} %get-tuple-element.24), channel_id=1, source_target_pairs={{0,16},{1,17},{2,18},{3,19},{4,6},{5,7},{6,4},{7,5},{8,24},{9,25},... | collective-permute-start | bytes 15368 | tf_op jit(solution)/shard_map/ppermute | solution.py:33
  31.5 2.1 %collective-permute-done.9.second_ref = f32[4,320]{1,0:T(4,128)S(1)} collective-permute-done((f32[4,320]{1,0:T(4,128)S(1)}, f32[4,320]{1,0:T(4,128)S(1)}, u32[]{:S(2)}, u32[]{:S(2)}) %collective-permute-start.9) | collective-permute-done | bytes 5152 | tf_op jit(solution)/shard_map/ppermute | solution.py:33
  33.6 0.0 collective-permute-done.8.first_ref
  33.6 0.6 %shard_map.40 = (f32[8,320]{1,0:T(8,128)S(1)}, f32[8,2688]{1,0:T(8,128)S(1)}) custom-call(f32[8,320]{1,0:T(8,128)S(1)} %add.35.images_ref, f32[4,320]{1,0:T(4,128)S(1)} %collective-permute-done.8.first_ref, f32[4,320]{1,0:T(4,128)S(1)} %collective-permute-done.9.second_ref, bf16[320,2560]{1,0:T(8,128)(2,1)S(1)} %get-tuple-element.15.replicas_ref, ...), custom_call_target="tpu_custom_call" | custom-call | tf_op jit(solution)/shard_map/pallas_call | solution.py:234
  34.2 0.1 collective-permute-start.10
  34.3 1.3 %collective-permute-done.10 = f32[8,2688]{1,0:T(8,128)S(1)} collective-permute-done((f32[8,2688]{1,0:T(8,128)S(1)}, f32[8,2688]{1,0:T(8,128)S(1)}, u32[]{:S(2)}, u32[]{:S(2)}) %collective-permute-start.10) | collective-permute-done | bytes 86048 | tf_op jit(solution)/shard_map/ppermute | solution.py:33
  35.6 1.3 %collective-permute-start.11 = (f32[4,2688]{1,0:T(4,128)S(1)}, f32[4,2688]{1,0:T(4,128)S(1)}, u32[]{:S(2)}, u32[]{:S(2)}) collective-permute-start(f32[4,2688]{1,0:T(4,128)S(1)} %slice_add_fusion), channel_id=1, source_target_pairs={{0,12},{1,13},{2,14},{3,15},{4,8},{5,9},{6,10},{7,11},{8,4},{9,5},... | collective-permute-start | bytes 129032 | tf_op jit(solution)/shard_map/ppermute | solution.py:33
  36.9 2.3 %collective-permute-done.11 = f32[4,2688]{1,0:T(4,128)S(1)} collective-permute-done((f32[4,2688]{1,0:T(4,128)S(1)}, f32[4,2688]{1,0:T(4,128)S(1)}, u32[]{:S(2)}, u32[]{:S(2)}) %collective-permute-start.11) | collective-permute-done | bytes 43040 | tf_op jit(solution)/shard_map/ppermute | solution.py:33
  39.2 1.6 %collective-permute-start.12 = (f32[4,2688]{1,0:T(4,128)S(1)}, f32[4,2688]{1,0:T(4,128)S(1)}, u32[]{:S(2)}, u32[]{:S(2)}) collective-permute-start(f32[4,2688]{1,0:T(4,128)S(1)} %fusion), channel_id=1, source_target_pairs={{0,16},{1,17},{2,18},{3,19},{4,6},{5,7},{6,4},{7,5},{8,24},{9,25},... | collective-permute-start | bytes 129032 | tf_op jit(solution)/shard_map/ppermute | solution.py:33
  40.8 2.5 %collective-permute-done.12 = f32[4,2688]{1,0:T(4,128)S(1)} collective-permute-done((f32[4,2688]{1,0:T(4,128)S(1)}, f32[4,2688]{1,0:T(4,128)S(1)}, u32[]{:S(2)}, u32[]{:S(2)}) %collective-permute-start.12) | collective-permute-done | bytes 43040 | tf_op jit(solution)/shard_map/ppermute | solution.py:33
  43.4 0.1 collective-permute-start.13
  43.4 1.2 %collective-permute-done.13.other_ref = f32[4,2688]{1,0:T(4,128)S(1)} collective-permute-done((f32[4,2688]{1,0:T(4,128)S(1)}, f32[4,2688]{1,0:T(4,128)S(1)}, u32[]{:S(2)}, u32[]{:S(2)}) %collective-permute-start.13) | collective-permute-done | bytes 43040 | tf_op jit(solution)/shard_map/ppermute | solution.py:33
  44.6 2.3 %shard_map.41 = f32[320,2560]{1,0:T(8,128)} custom-call(f32[4,2688]{1,0:T(4,128)S(1)} %add.39.mine_ref, f32[4,2688]{1,0:T(4,128)S(1)} %collective-permute-done.13.other_ref, f32[8,128]{1,0:T(8,128)S(1)} %get-tuple-element.17.scaling_ref, f32[8,320]{1,0:T(8,128)S(1)} %get-tuple-element.18.left_ref.refs_0_.first_ref, ...), custom_call_target="tpu_custom_call" | custom-call | tf_op jit(solution)/shard_map/pallas_call | solution.py:234
  (10 shorter events, 0.1 us)
Async XLA Ops:
  2.1 4.8 %collective-permute-start = (f32[8,320]{1,0:T(8,128)S(1)}, f32[8,320]{1,0:T(8,128)S(1)}, u32[]{:S(2)}, u32[]{:S(2)}) collective-permute-start(f32[8,320]{1,0:T(8,128)S(1)} %get-tuple-element.14), channel_id=1, source_target_pairs={{0,1},{1,0},{2,3},{3,2},{4,5},{5,4},{6,7},{7,6},{8,9},{9,8},{10,11... | collective-permute-start | bytes 30728 | tf_op jit(solution)/shard_map/ppermute | solution.py:33
  6.9 4.7 %collective-permute-start.2 = (f32[4,320]{1,0:T(4,128)S(1)}, f32[4,320]{1,0:T(4,128)S(1)}, u32[]{:S(2)}, u32[]{:S(2)}) collective-permute-start(f32[4,320]{1,0:T(4,128)S(1)} %get-tuple-element.25), channel_id=1, source_target_pairs={{0,2},{1,3},{2,0},{3,1},{4,20},{5,21},{6,22},{7,23},{8,10},{9,11},... | collective-permute-start | bytes 15368 | tf_op jit(solution)/shard_map/ppermute | solution.py:33
  10.0 3.6 %collective-permute-start.1 = (f32[4,320]{1,0:T(4,128)S(1)}, f32[4,320]{1,0:T(4,128)S(1)}, u32[]{:S(2)}, u32[]{:S(2)}) collective-permute-start(f32[4,320]{1,0:T(4,128)S(1)} %get-tuple-element.26), channel_id=1, source_target_pairs={{0,16},{1,17},{2,18},{3,19},{4,6},{5,7},{6,4},{7,5},{8,24},{9,25},... | collective-permute-start | bytes 15368 | tf_op jit(solution)/shard_map/ppermute | solution.py:33
  14.0 1.3 %collective-permute-start.3 = (f32[8,2688]{1,0:T(8,128)S(1)}, f32[8,2688]{1,0:T(8,128)S(1)}, u32[]{:S(2)}, u32[]{:S(2)}) collective-permute-start(f32[8,2688]{1,0:T(8,128)S(1)} %get-tuple-element.16), channel_id=1, source_target_pairs={{0,4},{1,5},{2,6},{3,7},{4,0},{5,1},{6,2},{7,3},{8,12},{9,13},{10,... | collective-permute-start | bytes 258056 | tf_op jit(solution)/shard_map/ppermute | solution.py:33
  15.3 3.6 %collective-permute-start.4 = (f32[4,2688]{1,0:T(4,128)S(1)}, f32[4,2688]{1,0:T(4,128)S(1)}, u32[]{:S(2)}, u32[]{:S(2)}) collective-permute-start(f32[4,2688]{1,0:T(4,128)S(1)} %slice_add_fusion.2), channel_id=1, source_target_pairs={{0,12},{1,13},{2,14},{3,15},{4,8},{5,9},{6,10},{7,11},{8,4},{9,5},... | collective-permute-start | bytes 129032 | tf_op jit(solution)/shard_map/ppermute | solution.py:33
  18.9 4.1 %collective-permute-start.5 = (f32[4,2688]{1,0:T(4,128)S(1)}, f32[4,2688]{1,0:T(4,128)S(1)}, u32[]{:S(2)}, u32[]{:S(2)}) collective-permute-start(f32[4,2688]{1,0:T(4,128)S(1)} %fusion.1), channel_id=1, source_target_pairs={{0,16},{1,17},{2,18},{3,19},{4,6},{5,7},{6,4},{7,5},{8,24},{9,25},... | collective-permute-start | bytes 129032 | tf_op jit(solution)/shard_map/ppermute | solution.py:33
  23.0 1.3 %collective-permute-start.6 = (f32[4,2688]{1,0:T(4,128)S(1)}, f32[4,2688]{1,0:T(4,128)S(1)}, u32[]{:S(2)}, u32[]{:S(2)}) collective-permute-start(f32[4,2688]{1,0:T(4,128)S(1)} %add.34.mine_ref), channel_id=1, source_target_pairs={{0,4},{1,5},{2,6},{3,7},{4,0},{5,1},{6,2},{7,3},{8,12},{9,13},{10,... | collective-permute-start | bytes 129032 | tf_op jit(solution)/shard_map/ppermute | solution.py:33
  25.3 3.7 %collective-permute-start.7 = (f32[8,320]{1,0:T(8,128)S(1)}, f32[8,320]{1,0:T(8,128)S(1)}, u32[]{:S(2)}, u32[]{:S(2)}) collective-permute-start(f32[8,320]{1,0:T(8,128)S(1)} %get-tuple-element.19), channel_id=1, source_target_pairs={{0,1},{1,0},{2,3},{3,2},{4,5},{5,4},{6,7},{7,6},{8,9},{9,8},{10,11... | collective-permute-start | bytes 30728 | tf_op jit(solution)/shard_map/ppermute | solution.py:33
  29.1 4.6 %collective-permute-start.9 = (f32[4,320]{1,0:T(4,128)S(1)}, f32[4,320]{1,0:T(4,128)S(1)}, u32[]{:S(2)}, u32[]{:S(2)}) collective-permute-start(f32[4,320]{1,0:T(4,128)S(1)} %get-tuple-element.23), channel_id=1, source_target_pairs={{0,2},{1,3},{2,0},{3,1},{4,20},{5,21},{6,22},{7,23},{8,10},{9,11},... | collective-permute-start | bytes 15368 | tf_op jit(solution)/shard_map/ppermute | solution.py:33
  30.0 3.6 %collective-permute-start.8 = (f32[4,320]{1,0:T(4,128)S(1)}, f32[4,320]{1,0:T(4,128)S(1)}, u32[]{:S(2)}, u32[]{:S(2)}) collective-permute-start(f32[4,320]{1,0:T(4,128)S(1)} %get-tuple-element.24), channel_id=1, source_target_pairs={{0,16},{1,17},{2,18},{3,19},{4,6},{5,7},{6,4},{7,5},{8,24},{9,25},... | collective-permute-start | bytes 15368 | tf_op jit(solution)/shard_map/ppermute | solution.py:33
  34.2 1.3 %collective-permute-start.10 = (f32[8,2688]{1,0:T(8,128)S(1)}, f32[8,2688]{1,0:T(8,128)S(1)}, u32[]{:S(2)}, u32[]{:S(2)}) collective-permute-start(f32[8,2688]{1,0:T(8,128)S(1)} %get-tuple-element.21), channel_id=1, source_target_pairs={{0,4},{1,5},{2,6},{3,7},{4,0},{5,1},{6,2},{7,3},{8,12},{9,13},{10,... | collective-permute-start | bytes 258056 | tf_op jit(solution)/shard_map/ppermute | solution.py:33
  35.6 3.6 %collective-permute-start.11 = (f32[4,2688]{1,0:T(4,128)S(1)}, f32[4,2688]{1,0:T(4,128)S(1)}, u32[]{:S(2)}, u32[]{:S(2)}) collective-permute-start(f32[4,2688]{1,0:T(4,128)S(1)} %slice_add_fusion), channel_id=1, source_target_pairs={{0,12},{1,13},{2,14},{3,15},{4,8},{5,9},{6,10},{7,11},{8,4},{9,5},... | collective-permute-start | bytes 129032 | tf_op jit(solution)/shard_map/ppermute | solution.py:33
  39.2 4.1 %collective-permute-start.12 = (f32[4,2688]{1,0:T(4,128)S(1)}, f32[4,2688]{1,0:T(4,128)S(1)}, u32[]{:S(2)}, u32[]{:S(2)}) collective-permute-start(f32[4,2688]{1,0:T(4,128)S(1)} %fusion), channel_id=1, source_target_pairs={{0,16},{1,17},{2,18},{3,19},{4,6},{5,7},{6,4},{7,5},{8,24},{9,25},... | collective-permute-start | bytes 129032 | tf_op jit(solution)/shard_map/ppermute | solution.py:33
  43.4 1.3 %collective-permute-start.13 = (f32[4,2688]{1,0:T(4,128)S(1)}, f32[4,2688]{1,0:T(4,128)S(1)}, u32[]{:S(2)}, u32[]{:S(2)}) collective-permute-start(f32[4,2688]{1,0:T(4,128)S(1)} %add.39.mine_ref), channel_id=1, source_target_pairs={{0,4},{1,5},{2,6},{3,7},{4,0},{5,1},{6,2},{7,3},{8,12},{9,13},{10,... | collective-permute-start | bytes 129032 | tf_op jit(solution)/shard_map/ppermute | solution.py:33

commit v4 on v3

--- a/solution.py
+++ b/solution.py
@@ -49,9 +49,10 @@
     def neighbours(self, value, half):
         if self.nodes == (2, 2):
             return self.exchange(value, self.step(half, 1))
-        after = self.exchange(value[2:], self.step(half, -1))
-        before = self.exchange(value[:2], self.step(half, 1))
-        return jnp.concatenate([after, before], 0)
+        fours = value.reshape(-1, 2, 2, value.shape[1])
+        after = self.exchange(fours[:, 1], self.step(half, -1))
+        before = self.exchange(fours[:, 0], self.step(half, 1))
+        return jnp.stack([after, before], 1).reshape(value.shape)
 
     def edges(self):
         row_index, col_index = lax.axis_index("row"), lax.axis_index("col")
@@ -110,7 +111,7 @@
 
 
 def first_kernel(
-    layout, seeds_hbm, counts_hbm, replicas_hbm, images_ref, scaling_ref, replicas_ref, seeds_ref, counts_ref, sems
+    layout, seeds_hbm, counts_hbm, replicas_hbm, keep_ref, send_ref, scaling_ref, replicas_ref, seeds_ref, counts_ref, sems
 ):
     size = replicas_ref.shape[1] // CHUNKS
     blocks = [pl.ds(k * size, size) for k in range(CHUNKS)]
@@ -140,29 +141,57 @@
     for k, block in enumerate(blocks):
         copies[k].wait()
         images = images + dot(factors[:, k * size : (k + 1) * size], replicas_ref[:, block], over_last)
-    images_ref[...] = folded(images)
-
-
-def project_kernel(has_update, images_ref, first_ref, second_ref, replicas_ref, *refs):
+    images = folded(images)
+    keep_ref[...] = images[0:4]
+    send_ref[...] = images[4:8]
+
+
+def widen_kernel(values_ref, out_ref):
+    out_ref[...] = values_ref[...].astype(jnp.float32)
+
+
+def narrow_kernel(values_ref, out_ref):
+    out_ref[...] = values_ref[...].astype(jnp.bfloat16)
+
+
+def upper(shape):
+    return lax.broadcasted_iota(jnp.int32, shape, 0) < 4
+
+
+def halves_added(values):
+    return values + pltpu.roll(values, 4, 0)
+
+
+def project_kernel(has_update, images_ref, neighbour_ref, mine_ref, pair_ref, *refs):
     if has_update:
-        earlier_ref, right_ref, left_ref, packed_ref = refs
+        mine_left_ref, pair_left_ref, right_ref, left_ref, packed_ref, wide_ref = refs
     else:
-        left_ref, packed_ref = refs
-    left_ref[0:4] = images_ref[0:4] - first_ref[...]
-    left_ref[4:8] = images_ref[4:8] - second_ref[...]
-    left = left_ref[...]
-    width = replicas_ref.shape[1]
-    projections = folded(dot(stacked(left), replicas_ref[...], over_inner))
+        left_ref, packed_ref, wide_ref = refs
+    left = images_ref[...] - neighbour_ref[...]
+    left_ref[...] = left
+    height, width = mine_ref.shape
+    wide_ref[:, :height] = left[0:4]
+    wide_ref[:, wide_ref.shape[1] // 2 : wide_ref.shape[1] // 2 + height] = left[4:8]
+    terms = stacked(left)
+    projections = jnp.where(
+        upper((8, width)),
+        folded(dot(terms, mine_ref[...], over_inner)),
+        folded(dot(terms, pair_ref[...], over_inner)),
+    )
     if has_update:
-        cross = full_product(left, earlier_ref[...], over_last)
+        cross = jnp.where(
+            upper((8, 8)),
+            full_product(left, mine_left_ref[...], over_last),
+            full_product(left, pair_left_ref[...], over_last),
+        )
         projections = projections + full_product(cross, right_ref[...], over_inner)
     rows = lax.broadcasted_iota(jnp.int32, left.shape, 0)
     partner = jnp.where(rows % 2 == 0, pltpu.roll(left, 7, 0), pltpu.roll(left, 1, 0))
     norm = jnp.sum(left * left, 1, keepdims=True)
     inner = jnp.sum(left * partner, 1, keepdims=True)
     lanes = lax.broadcasted_iota(jnp.int32, (8, LANES), 1)
-    packed_ref[:, :width] = projections
-    packed_ref[:, width:] = jnp.where(lanes == 0, norm, inner)
+    packed_ref[:, :width] = halves_added(projections)[0:4]
+    packed_ref[:, width:] = halves_added(jnp.where(lanes == 0, norm, inner))[0:4]
 
 
 def coefficients(total_ref, width):
@@ -188,25 +217,59 @@
     return factors, scaling * (own * factors + from_after * pltpu.roll(factors, 7, 0))
 
 
-def images_kernel(mine_ref, other_ref, scaling_ref, left_ref, replicas_ref, images_ref, right_ref, total_ref):
-    total_ref[0:4] = mine_ref[...]
-    total_ref[4:8] = other_ref[...]
+def own_kernel(mine_ref, scaling_ref, replicas_ref, pair_ref, images_ref, factors_ref, right_ref, total_ref):
     width = replicas_ref.shape[1]
+    total_ref[0:4] = mine_ref[:, : width + LANES]
+    total_ref[4:8] = mine_ref[:, : width + LANES]
     factors, right = right_factors(
         total_ref[:, :width], scaling_ref[:, 0:1], *coefficients(total_ref, width)
     )
-    right_ref[...] = right
-    images = folded(dot(stacked(factors), replicas_ref[...], over_last))
-    cross = full_product(factors, right, over_last)
-    images_ref[...] = images + full_product(cross, left_ref[...], over_inner)
+    factors_ref[...] = factors
+    right_ref[...] = right[0:4]
+    high = factors.astype(jnp.bfloat16).astype(jnp.float32)
+    terms = jnp.where(upper(factors.shape), high, factors - high).astype(jnp.bfloat16)
+    images = halves_added(dot(terms, replicas_ref[...], over_last))
+    pair_images = halves_added(dot(terms, pair_ref[...], over_last))
+    images_ref[...] = jnp.where(upper(images.shape), images, pair_images)
+
+
+def images_kernel(
+    other_ref, scaling_ref, left_ref, partial_ref, factors_ref, own_right_ref,
+    images_ref, mine_left_ref, pair_left_ref, right_ref, total_ref,
+):
+    height, width = left_ref.shape[1], factors_ref.shape[1]
+    total_ref[0:4] = other_ref[:, : width + LANES]
+    total_ref[4:8] = other_ref[:, : width + LANES]
+    _, right = right_factors(
+        total_ref[:, :width], scaling_ref[:, 0:1], *coefficients(total_ref, width)
+    )
+    right_ref[0:4] = own_right_ref[...]
+    right_ref[4:8] = right[4:8]
+    first = width + LANES
+    second = first + (other_ref.shape[1] - first) // 2
+    mine_left_ref[0:4] = left_ref[0:4]
+    mine_left_ref[4:8] = other_ref[:, second : second + height]
+    pair_left_ref[0:4] = left_ref[4:8]
+    pair_left_ref[4:8] = other_ref[:, first : first + height]
+    cross = full_product(factors_ref[...], right_ref[...], over_last)
+    images_ref[...] = partial_ref[...] + jnp.where(
+        upper((8, height)),
+        full_product(cross, mine_left_ref[...], over_inner),
+        full_product(cross, pair_left_ref[...], over_inner),
+    )
 
 
 def update_kernel(
-    mine_ref, other_ref, scaling_ref, first_ref, second_ref, right_ref, out_ref, total_ref, block_ref, sems
+    mine_ref, other_ref, scaling_ref, first_ref, left_ref, right_ref, out_ref, total_ref, second_ref, block_ref, sems
 ):
-    total_ref[0:4] = mine_ref[...]
-    total_ref[4:8] = other_ref[...]
-    parts = coefficients(total_ref, right_ref.shape[1])
+    height, width = left_ref.shape[1], right_ref.shape[1]
+    packed = width + LANES
+    total_ref[0:4] = mine_ref[:, :packed]
+    total_ref[4:8] = other_ref[:, :packed]
+    start = packed + (other_ref.shape[1] - packed) // 2
+    second_ref[0:4] = left_ref[0:4]
+    second_ref[4:8] = other_ref[:, start : start + height]
+    parts = coefficients(total_ref, width)
     scaling = scaling_ref[:, 0:1]
     lefts = jnp.concatenate([first_ref[...], second_ref[...]], 0)
     left_high = lefts.astype(jnp.bfloat16).astype(jnp.float32)
@@ -230,7 +293,7 @@
 hbm = pl.BlockSpec(memory_space=pltpu.HBM)
 
 
-def call(kernel, outs, *args, in_specs=None, out_specs=None, scratch=()):
+def call(kernel, outs, *args, in_specs=None, out_specs=None, scratch=(), work=0):
     return pl.pallas_call(
         kernel,
         out_shape=outs,
@@ -238,6 +301,7 @@
         out_specs=out_specs or [vmem] * len(outs),
         scratch_shapes=list(scratch),
         compiler_params=pltpu.CompilerParams(vmem_limit_bytes=16 << 20),
+        cost_estimate=pl.CostEstimate(flops=work, bytes_accessed=work, transcendentals=0),
     )(*args)
 
 
@@ -248,72 +312,107 @@
 def per_device(replicas_hbm, factor_seeds, edge_counts):
     height, width = replicas_hbm.shape
     packed = width + LANES
+    wide = 2 * (-(-height // LANES) * LANES)
     layout = Layout(*factor_seeds.shape[:2])
     total_scratch = pltpu.VMEM((8, packed), jnp.float32)
+    work = replicas_hbm.size
 
     def reduced(images):
         for bit in range(layout.shards[1].bit_length() - 1):
             images = images + layout.col_swap(images, bit)
-        return images, layout.neighbours(images[:4], 0), layout.neighbours(images[4:], 1)
-
-    def summed(values):
-        other = layout.row_swap(values, 0)
-        total, rest = values[:4] + other[4:], values[4:] + other[:4]
-        if layout.shards[0] > 2:
-            total = total + layout.exchange(rest, lambda r, c: (r ^ 3, c))
-        for bit in range(2, layout.shards[0].bit_length() - 1):
+        return images, layout.neighbours(images, 0)
+
+    def summed(total, left):
+        for bit in range(1, layout.shards[0].bit_length() - 1):
             total = total + layout.row_swap(total, bit)
-        total = total + layout.neighbours(total, 0)
+        total = jnp.concatenate([total + layout.neighbours(total, 0), left], 1)
         return total, layout.row_swap(total, 0)
 
-    images, scaling, replicas = call(
+    keep, send, scaling, replicas = call(
         functools.partial(first_kernel, layout),
-        [single(8, height), single(8, LANES), jax.ShapeDtypeStruct((height, width), replicas_hbm.dtype)],
-        *(pltpu.with_memory_space_constraint(array, pltpu.HBM) for array in (factor_seeds, edge_counts, replicas_hbm)),
+        [
+            single(4, height),
+            single(4, height),
+            single(8, LANES),
+            jax.ShapeDtypeStruct((height, width), replicas_hbm.dtype),
+        ],
+        *(
+            pltpu.with_memory_space_constraint(array, pltpu.HBM)
+            for array in (factor_seeds, edge_counts, replicas_hbm)
+        ),
         in_specs=[hbm] * 3,
         scratch=[
             pltpu.SMEM(factor_seeds.shape, jnp.int32),
             pltpu.SMEM(edge_counts.shape, jnp.int32),
             pltpu.SemaphoreType.DMA((CHUNKS + 2,)),
         ],
-    )
-    left_one, values = call(
+        work=work,
+    )
+    images = jnp.concatenate([keep, layout.row_swap(send, 0)], 0)
+    (widened,) = call(widen_kernel, [single(height, width)], replicas, work=work)
+    images, widened = lax.optimization_barrier((images, widened))
+    swapped = layout.row_swap(widened, 0)
+    (pair,) = call(
+        narrow_kernel, [jax.ShapeDtypeStruct((height, width), replicas_hbm.dtype)], swapped, work=work
+    )
+    left_one, values, wide_left = call(
         functools.partial(project_kernel, False),
-        [single(8, height), single(8, packed)],
+        [single(8, height), single(4, packed), single(4, wide)],
         *reduced(images),
         replicas,
-    )
-    images, right_one = call(
+        pair,
+        work=work,
+    )
+    mine, other = summed(values, wide_left)
+    partial, factors, right_one = call(
+        own_kernel,
+        [single(8, height), single(8, width), single(4, width)],
+        mine,
+        scaling,
+        replicas,
+        pair,
+        scratch=[total_scratch],
+        work=work,
+    )
+    images, mine_left, pair_left, right_one = call(
         images_kernel,
-        [single(8, height), single(8, width)],
-        *summed(values),
+        [single(8, height), single(8, height), single(8, height), single(8, width)],
+        other,
         scaling,
         left_one,
-        replicas,
+        partial,
+        factors,
+        right_one,
         scratch=[total_scratch],
-    )
-    left_two, values = call(
+        work=work,
+    )
+    left_two, values, wide_left = call(
         functools.partial(project_kernel, True),
-        [single(8, height), single(8, packed)],
+        [single(8, height), single(4, packed), single(4, wide)],
         *reduced(images),
         replicas,
-        left_one,
+        pair,
+        mine_left,
+        pair_left,
         right_one,
+        work=work,
     )
     (update,) = call(
         update_kernel,
         [single(height, width)],
-        *summed(values),
+        *summed(values, wide_left),
         scaling,
-        left_one,
+        mine_left,
         left_two,
         right_one,
         out_specs=[hbm],
         scratch=[
             total_scratch,
+            pltpu.VMEM((8, height), jnp.float32),
             pltpu.VMEM((CHUNKS, height, width // CHUNKS), jnp.float32),
             pltpu.SemaphoreType.DMA((CHUNKS,)),
         ],
+        work=work,
     )
     return update
 

time: 47.1 us -> 43.1 us (0.915)
  waiting for transfers between devices: 22.6 us -> 16.8 us
  Pallas kernels: 6.24 us -> 8.11 us
    ppermute x14 -> x12, waiting for transfers between devices: 22.6 us -> 16.8 us  [exchange(): return lax.ppermute(value, ('row', 'col'), pairs)]
    pallas_call x5 -> x8, Pallas kernels: 6.24 us -> 8.11 us  [call(): pl.pallas_call(kernel, out_shape=outs, in_specs=in_specs or [vmem] * len(...]
    ppermute x14 -> x12, starting transfers between devices: 17.8 us -> 17.9 us  [exchange(): return lax.ppermute(value, ('row', 'col'), pairs)]
  transfers between devices with their start and end apart: 14 -> 12, of which waited for: 13 -> 10; matrix products, arithmetic and copies ran while one was open for 0% -> 0% of each run, Pallas kernels for 0% -> 4%
where the time goes in v4:
time: 43.1 us; the launch traced here: 43 us
  starting transfers between devices  17.9 us (42%)
  waiting for transfers between devices  16.8 us (39%)
  Pallas kernels  8.11 us (19%)
    ppermute x12, starting transfers between devices, exchange(): return lax.ppermute(value, ('row', 'col'), pairs)  17.9 us
    ppermute x12, waiting for transfers between devices, exchange(): return lax.ppermute(value, ('row', 'col'), pairs)  16.8 us
    pallas_call x8, Pallas kernels, call(): pl.pallas_call(kernel, out_shape=outs, in_specs=in_specs or [vmem] * len(...  8.11 us
  transfers between devices with their start and end apart: 12, of which 10 were waited for; matrix products, arithmetic and copies ran while one was open for 0% of the time, Pallas kernels for 4%

profile of v4, /device:TPU:0, one launch (start us, length us, event | category | flops | bytes accessed | tf_op | source)
XLA Modules:
  0.0 43.0 jit_solution(15619725674440471059)
XLA Ops:
  0.0 2.1 %shard_map.37 = (f32[4,320]{1,0:T(4,128)S(1)}, f32[4,320]{1,0:T(4,128)S(1)}, f32[8,128]{1,0:T(8,128)S(1)}, bf16[320,2560]{1,0:T(8,128)(2,1)S(1)}) custom-call(s32[2,2,2,2]{3,2,1,0:T(2,128)} %seeds_hbm.1, s32[2,2,2]{2,1,0:T(2,128)} %counts_hbm.1, bf16[320,2560]{1,0:T(8,128)(2,1)} %replicas_hbm.1), custom_call_target="tpu_custom_call" | custom-call | flops 819200 | bytes 819200 | tf_op jit(solution)/shard_map/pallas_call | solution.py:297
  2.1 0.6 %collective-permute-start = (f32[4,320]{1,0:T(4,128)S(1)}, f32[4,320]{1,0:T(4,128)S(1)}, u32[]{:S(2)}, u32[]{:S(2)}) collective-permute-start(f32[4,320]{1,0:T(4,128)S(1)} %get-tuple-element.25), channel_id=1, source_target_pairs={{0,4},{1,5},{2,6},{3,7},{4,0},{5,1},{6,2},{7,3},{8,12},{9,13},{10,... | collective-permute-start | bytes 15368 | tf_op jit(solution)/shard_map/ppermute | solution.py:33
  2.6 0.2 shard_map.38
  2.9 0.6 %collective-permute-done = f32[4,320]{1,0:T(4,128)S(1)} collective-permute-done((f32[4,320]{1,0:T(4,128)S(1)}, f32[4,320]{1,0:T(4,128)S(1)}, u32[]{:S(2)}, u32[]{:S(2)}) %collective-permute-start) | collective-permute-done | bytes 5152 | tf_op jit(solution)/shard_map/ppermute | solution.py:33
  3.5 0.4 collective-permute-start.3
  3.9 2.7 %collective-permute-start.1 = (f32[8,320]{1,0:T(8,128)S(1)}, f32[8,320]{1,0:T(8,128)S(1)}, u32[]{:S(2)}, u32[]{:S(2)}) collective-permute-start(f32[8,320]{1,0:T(8,128)S(1)} %pad_maximum_fusion.2), channel_id=1, source_target_pairs={{0,1},{1,0},{2,3},{3,2},{4,5},{5,4},{6,7},{7,6},{8,9},{9,8},{10,11... | collective-permute-start | bytes 30728 | tf_op jit(solution)/shard_map/ppermute | solution.py:33
  6.6 1.7 %collective-permute-done.1 = f32[8,320]{1,0:T(8,128)S(1)} collective-permute-done((f32[8,320]{1,0:T(8,128)S(1)}, f32[8,320]{1,0:T(8,128)S(1)}, u32[]{:S(2)}, u32[]{:S(2)}) %collective-permute-start.1) | collective-permute-done | bytes 10272 | tf_op jit(solution)/shard_map/ppermute | solution.py:33
  8.3 2.0 %collective-permute-start.2 = (f32[8,320]{1,0:T(8,128)S(1)}, f32[8,320]{1,0:T(8,128)S(1)}, u32[]{:S(2)}, u32[]{:S(2)}) collective-permute-start(f32[8,320]{1,0:T(8,128)S(1)} %add.18.images_ref), channel_id=1, source_target_pairs={{0,16},{1,17},{2,18},{3,19},{4,6},{5,7},{6,4},{7,5},{8,24},{9,25},... | collective-permute-start | bytes 30728 | tf_op jit(solution)/shard_map/ppermute | solution.py:33
  10.3 0.0 collective-permute-done.3.values_ref
  10.3 0.2 shard_map.39.pair_ref
  10.4 1.6 %collective-permute-done.2.neighbour_ref = f32[8,320]{1,0:T(8,128)S(1)} collective-permute-done((f32[8,320]{1,0:T(8,128)S(1)}, f32[8,320]{1,0:T(8,128)S(1)}, u32[]{:S(2)}, u32[]{:S(2)}) %collective-permute-start.2) | collective-permute-done | bytes 10272 | tf_op jit(solution)/shard_map/ppermute | solution.py:33
  12.0 0.6 %shard_map.40 = (f32[8,320]{1,0:T(8,128)S(1)}, f32[4,2688]{1,0:T(4,128)S(1)}, f32[4,768]{1,0:T(4,128)S(1)}) custom-call(f32[8,320]{1,0:T(8,128)S(1)} %add.18.images_ref, f32[8,320]{1,0:T(8,128)S(1)} %collective-permute-done.2.neighbour_ref, bf16[320,2560]{1,0:T(8,128)(2,1)S(1)} %get-tuple-element.26.values_ref.mine_ref.replicas_ref, ...), custom_call_target="tpu_custom_call" | custom-call | flops 819200 | bytes 819200 | tf_op jit(solution)/shard_map/pallas_call | solution.py:297
  12.6 2.0 %collective-permute-start.4 = (f32[4,2688]{1,0:T(4,128)S(1)}, f32[4,2688]{1,0:T(4,128)S(1)}, u32[]{:S(2)}, u32[]{:S(2)}) collective-permute-start(f32[4,2688]{1,0:T(4,128)S(1)} %get-tuple-element.29), channel_id=1, source_target_pairs={{0,8},{1,9},{2,10},{3,11},{4,12},{5,13},{6,14},{7,15},{8,0},{9,1},... | collective-permute-start | bytes 129032 | tf_op jit(solution)/shard_map/ppermute | solution.py:33
  14.6 2.1 %collective-permute-done.4 = f32[4,2688]{1,0:T(4,128)S(1)} collective-permute-done((f32[4,2688]{1,0:T(4,128)S(1)}, f32[4,2688]{1,0:T(4,128)S(1)}, u32[]{:S(2)}, u32[]{:S(2)}) %collective-permute-start.4) | collective-permute-done | bytes 43040 | tf_op jit(solution)/shard_map/ppermute | solution.py:33
  16.7 2.0 %collective-permute-start.5 = (f32[4,2688]{1,0:T(4,128)S(1)}, f32[4,2688]{1,0:T(4,128)S(1)}, u32[]{:S(2)}, u32[]{:S(2)}) collective-permute-start(f32[4,2688]{1,0:T(4,128)S(1)} %add.19), channel_id=1, source_target_pairs={{0,16},{1,17},{2,18},{3,19},{4,6},{5,7},{6,4},{7,5},{8,24},{9,25},... | collective-permute-start | bytes 129032 | tf_op jit(solution)/shard_map/ppermute | solution.py:33
  18.7 2.1 %collective-permute-done.5 = f32[4,2688]{1,0:T(4,128)S(1)} collective-permute-done((f32[4,2688]{1,0:T(4,128)S(1)}, f32[4,2688]{1,0:T(4,128)S(1)}, u32[]{:S(2)}, u32[]{:S(2)}) %collective-permute-start.5) | collective-permute-done | bytes 43040 | tf_op jit(solution)/shard_map/ppermute | solution.py:33
  20.8 0.1 collective-permute-start.6
  20.9 1.2 %shard_map.41 = (f32[8,320]{1,0:T(8,128)S(1)}, f32[8,2560]{1,0:T(8,128)S(1)}, f32[4,2560]{1,0:T(4,128)S(1)}) custom-call(f32[4,3456]{1,0:T(4,128)S(1)} %pad_maximum_fusion.mine_ref, f32[8,128]{1,0:T(8,128)S(1)} %get-tuple-element.31.scaling_ref, bf16[320,2560]{1,0:T(8,128)(2,1)S(1)} %get-tuple-element.26.values_ref.mine_ref.replicas_ref, ...), custom_call_target="tpu_custom_call" | custom-call | flops 819200 | bytes 819200 | tf_op jit(solution)/shard_map/pallas_call | solution.py:297
  22.1 0.0 collective-permute-done.6.other_ref
  22.1 0.7 %shard_map.42 = (f32[8,320]{1,0:T(8,128)S(1)}, f32[8,320]{1,0:T(8,128)S(1)}, f32[8,320]{1,0:T(8,128)S(1)}, f32[8,2560]{1,0:T(8,128)S(1)}) custom-call(f32[4,3456]{1,0:T(4,128)S(1)} %collective-permute-done.6.other_ref, f32[8,128]{1,0:T(8,128)S(1)} %get-tuple-element.31.scaling_ref, f32[8,320]{1,0:T(8,128)S(1)} %get-tuple-element.32.left_ref, ...), custom_call_target="tpu_custom_call" | custom-call | flops 819200 | bytes 819200 | tf_op jit(solution)/shard_map/pallas_call | solution.py:297
  22.8 2.1 %collective-permute-start.7 = (f32[8,320]{1,0:T(8,128)S(1)}, f32[8,320]{1,0:T(8,128)S(1)}, u32[]{:S(2)}, u32[]{:S(2)}) collective-permute-start(f32[8,320]{1,0:T(8,128)S(1)} %get-tuple-element.36), channel_id=1, source_target_pairs={{0,1},{1,0},{2,3},{3,2},{4,5},{5,4},{6,7},{7,6},{8,9},{9,8},{10,11... | collective-permute-start | bytes 30728 | tf_op jit(solution)/shard_map/ppermute | solution.py:33
  24.9 1.7 %collective-permute-done.7 = f32[8,320]{1,0:T(8,128)S(1)} collective-permute-done((f32[8,320]{1,0:T(8,128)S(1)}, f32[8,320]{1,0:T(8,128)S(1)}, u32[]{:S(2)}, u32[]{:S(2)}) %collective-permute-start.7) | collective-permute-done | bytes 10272 | tf_op jit(solution)/shard_map/ppermute | solution.py:33
  26.6 2.0 %collective-permute-start.8 = (f32[8,320]{1,0:T(8,128)S(1)}, f32[8,320]{1,0:T(8,128)S(1)}, u32[]{:S(2)}, u32[]{:S(2)}) collective-permute-start(f32[8,320]{1,0:T(8,128)S(1)} %add.21.images_ref), channel_id=1, source_target_pairs={{0,16},{1,17},{2,18},{3,19},{4,6},{5,7},{6,4},{7,5},{8,24},{9,25},... | collective-permute-start | bytes 30728 | tf_op jit(solution)/shard_map/ppermute | solution.py:33
  28.6 1.7 %collective-permute-done.8.neighbour_ref = f32[8,320]{1,0:T(8,128)S(1)} collective-permute-done((f32[8,320]{1,0:T(8,128)S(1)}, f32[8,320]{1,0:T(8,128)S(1)}, u32[]{:S(2)}, u32[]{:S(2)}) %collective-permute-start.8) | collective-permute-done | bytes 10272 | tf_op jit(solution)/shard_map/ppermute | solution.py:33
  30.3 0.8 %shard_map.43 = (f32[8,320]{1,0:T(8,128)S(1)}, f32[4,2688]{1,0:T(4,128)S(1)}, f32[4,768]{1,0:T(4,128)S(1)}) custom-call(f32[8,320]{1,0:T(8,128)S(1)} %add.21.images_ref, f32[8,320]{1,0:T(8,128)S(1)} %collective-permute-done.8.neighbour_ref, bf16[320,2560]{1,0:T(8,128)(2,1)S(1)} %get-tuple-element.26.values_ref.mine_ref.replicas_ref, ...), custom_call_target="tpu_custom_call" | custom-call | flops 819200 | bytes 819200 | tf_op jit(solution)/shard_map/pallas_call | solution.py:297
  31.1 2.0 %collective-permute-start.9 = (f32[4,2688]{1,0:T(4,128)S(1)}, f32[4,2688]{1,0:T(4,128)S(1)}, u32[]{:S(2)}, u32[]{:S(2)}) collective-permute-start(f32[4,2688]{1,0:T(4,128)S(1)} %get-tuple-element.40), channel_id=1, source_target_pairs={{0,8},{1,9},{2,10},{3,11},{4,12},{5,13},{6,14},{7,15},{8,0},{9,1},... | collective-permute-start | bytes 129032 | tf_op jit(solution)/shard_map/ppermute | solution.py:33
  33.1 2.1 %collective-permute-done.9 = f32[4,2688]{1,0:T(4,128)S(1)} collective-permute-done((f32[4,2688]{1,0:T(4,128)S(1)}, f32[4,2688]{1,0:T(4,128)S(1)}, u32[]{:S(2)}, u32[]{:S(2)}) %collective-permute-start.9) | collective-permute-done | bytes 43040 | tf_op jit(solution)/shard_map/ppermute | solution.py:33
  35.2 2.0 %collective-permute-start.10 = (f32[4,2688]{1,0:T(4,128)S(1)}, f32[4,2688]{1,0:T(4,128)S(1)}, u32[]{:S(2)}, u32[]{:S(2)}) collective-permute-start(f32[4,2688]{1,0:T(4,128)S(1)} %add.22), channel_id=1, source_target_pairs={{0,16},{1,17},{2,18},{3,19},{4,6},{5,7},{6,4},{7,5},{8,24},{9,25},... | collective-permute-start | bytes 129032 | tf_op jit(solution)/shard_map/ppermute | solution.py:33
  37.3 2.1 %collective-permute-done.10 = f32[4,2688]{1,0:T(4,128)S(1)} collective-permute-done((f32[4,2688]{1,0:T(4,128)S(1)}, f32[4,2688]{1,0:T(4,128)S(1)}, u32[]{:S(2)}, u32[]{:S(2)}) %collective-permute-start.10) | collective-permute-done | bytes 43040 | tf_op jit(solution)/shard_map/ppermute | solution.py:33
  39.4 0.1 collective-permute-start.11
  39.4 1.2 %collective-permute-done.11.other_ref = f32[4,3456]{1,0:T(4,128)S(1)} collective-permute-done((f32[4,3456]{1,0:T(4,128)S(1)}, f32[4,3456]{1,0:T(4,128)S(1)}, u32[]{:S(2)}, u32[]{:S(2)}) %collective-permute-start.11) | collective-permute-done | bytes 55328 | tf_op jit(solution)/shard_map/ppermute | solution.py:33
  40.7 2.3 %shard_map.44 = f32[320,2560]{1,0:T(8,128)} custom-call(f32[4,3456]{1,0:T(4,128)S(1)} %pad_maximum_fusion.1.mine_ref, f32[4,3456]{1,0:T(4,128)S(1)} %collective-permute-done.11.other_ref, f32[8,128]{1,0:T(8,128)S(1)} %get-tuple-element.31.scaling_ref, f32[8,320]{1,0:T(8,128)S(1)} %get-tuple-element.37.refs_0_.first_ref, ...), custom_call_target="tpu_custom_call" | custom-call | flops 819200 | bytes 819200 | tf_op jit(solution)/shard_map/pallas_call | solution.py:297
  (9 shorter events, 0.1 us)
Async XLA Ops:
  2.1 1.4 %collective-permute-start = (f32[4,320]{1,0:T(4,128)S(1)}, f32[4,320]{1,0:T(4,128)S(1)}, u32[]{:S(2)}, u32[]{:S(2)}) collective-permute-start(f32[4,320]{1,0:T(4,128)S(1)} %get-tuple-element.25), channel_id=1, source_target_pairs={{0,4},{1,5},{2,6},{3,7},{4,0},{5,1},{6,2},{7,3},{8,12},{9,13},{10,... | collective-permute-start | bytes 15368 | tf_op jit(solution)/shard_map/ppermute | solution.py:33
  3.5 6.8 %collective-permute-start.3 = (f32[320,2560]{1,0:T(8,128)S(1)}, f32[320,2560]{1,0:T(8,128)S(1)}, u32[]{:S(2)}, u32[]{:S(2)}) collective-permute-start(f32[320,2560]{1,0:T(8,128)S(1)} %shard_map.38), channel_id=1, source_target_pairs={{0,4},{1,5},{2,6},{3,7},{4,0},{5,1},{6,2},{7,3},{8,12},{9,13},{10,... | collective-permute-start | bytes 9830408 | tf_op jit(solution)/shard_map/ppermute | solution.py:33
  3.9 4.4 %collective-permute-start.1 = (f32[8,320]{1,0:T(8,128)S(1)}, f32[8,320]{1,0:T(8,128)S(1)}, u32[]{:S(2)}, u32[]{:S(2)}) collective-permute-start(f32[8,320]{1,0:T(8,128)S(1)} %pad_maximum_fusion.2), channel_id=1, source_target_pairs={{0,1},{1,0},{2,3},{3,2},{4,5},{5,4},{6,7},{7,6},{8,9},{9,8},{10,11... | collective-permute-start | bytes 30728 | tf_op jit(solution)/shard_map/ppermute | solution.py:33
  8.3 3.7 %collective-permute-start.2 = (f32[8,320]{1,0:T(8,128)S(1)}, f32[8,320]{1,0:T(8,128)S(1)}, u32[]{:S(2)}, u32[]{:S(2)}) collective-permute-start(f32[8,320]{1,0:T(8,128)S(1)} %add.18.images_ref), channel_id=1, source_target_pairs={{0,16},{1,17},{2,18},{3,19},{4,6},{5,7},{6,4},{7,5},{8,24},{9,25},... | collective-permute-start | bytes 30728 | tf_op jit(solution)/shard_map/ppermute | solution.py:33
  12.6 4.1 %collective-permute-start.4 = (f32[4,2688]{1,0:T(4,128)S(1)}, f32[4,2688]{1,0:T(4,128)S(1)}, u32[]{:S(2)}, u32[]{:S(2)}) collective-permute-start(f32[4,2688]{1,0:T(4,128)S(1)} %get-tuple-element.29), channel_id=1, source_target_pairs={{0,8},{1,9},{2,10},{3,11},{4,12},{5,13},{6,14},{7,15},{8,0},{9,1},... | collective-permute-start | bytes 129032 | tf_op jit(solution)/shard_map/ppermute | solution.py:33
  16.7 4.1 %collective-permute-start.5 = (f32[4,2688]{1,0:T(4,128)S(1)}, f32[4,2688]{1,0:T(4,128)S(1)}, u32[]{:S(2)}, u32[]{:S(2)}) collective-permute-start(f32[4,2688]{1,0:T(4,128)S(1)} %add.19), channel_id=1, source_target_pairs={{0,16},{1,17},{2,18},{3,19},{4,6},{5,7},{6,4},{7,5},{8,24},{9,25},... | collective-permute-start | bytes 129032 | tf_op jit(solution)/shard_map/ppermute | solution.py:33
  20.8 1.3 %collective-permute-start.6 = (f32[4,3456]{1,0:T(4,128)S(1)}, f32[4,3456]{1,0:T(4,128)S(1)}, u32[]{:S(2)}, u32[]{:S(2)}) collective-permute-start(f32[4,3456]{1,0:T(4,128)S(1)} %pad_maximum_fusion.mine_ref), channel_id=1, source_target_pairs={{0,4},{1,5},{2,6},{3,7},{4,0},{5,1},{6,2},{7,3},{8,12},{9,13},{10,... | collective-permute-start | bytes 165896 | tf_op jit(solution)/shard_map/ppermute | solution.py:33
  22.8 3.8 %collective-permute-start.7 = (f32[8,320]{1,0:T(8,128)S(1)}, f32[8,320]{1,0:T(8,128)S(1)}, u32[]{:S(2)}, u32[]{:S(2)}) collective-permute-start(f32[8,320]{1,0:T(8,128)S(1)} %get-tuple-element.36), channel_id=1, source_target_pairs={{0,1},{1,0},{2,3},{3,2},{4,5},{5,4},{6,7},{7,6},{8,9},{9,8},{10,11... | collective-permute-start | bytes 30728 | tf_op jit(solution)/shard_map/ppermute | solution.py:33
  26.6 3.7 %collective-permute-start.8 = (f32[8,320]{1,0:T(8,128)S(1)}, f32[8,320]{1,0:T(8,128)S(1)}, u32[]{:S(2)}, u32[]{:S(2)}) collective-permute-start(f32[8,320]{1,0:T(8,128)S(1)} %add.21.images_ref), channel_id=1, source_target_pairs={{0,16},{1,17},{2,18},{3,19},{4,6},{5,7},{6,4},{7,5},{8,24},{9,25},... | collective-permute-start | bytes 30728 | tf_op jit(solution)/shard_map/ppermute | solution.py:33
  31.1 4.1 %collective-permute-start.9 = (f32[4,2688]{1,0:T(4,128)S(1)}, f32[4,2688]{1,0:T(4,128)S(1)}, u32[]{:S(2)}, u32[]{:S(2)}) collective-permute-start(f32[4,2688]{1,0:T(4,128)S(1)} %get-tuple-element.40), channel_id=1, source_target_pairs={{0,8},{1,9},{2,10},{3,11},{4,12},{5,13},{6,14},{7,15},{8,0},{9,1},... | collective-permute-start | bytes 129032 | tf_op jit(solution)/shard_map/ppermute | solution.py:33
  35.2 4.1 %collective-permute-start.10 = (f32[4,2688]{1,0:T(4,128)S(1)}, f32[4,2688]{1,0:T(4,128)S(1)}, u32[]{:S(2)}, u32[]{:S(2)}) collective-permute-start(f32[4,2688]{1,0:T(4,128)S(1)} %add.22), channel_id=1, source_target_pairs={{0,16},{1,17},{2,18},{3,19},{4,6},{5,7},{6,4},{7,5},{8,24},{9,25},... | collective-permute-start | bytes 129032 | tf_op jit(solution)/shard_map/ppermute | solution.py:33
  39.4 1.3 %collective-permute-start.11 = (f32[4,3456]{1,0:T(4,128)S(1)}, f32[4,3456]{1,0:T(4,128)S(1)}, u32[]{:S(2)}, u32[]{:S(2)}) collective-permute-start(f32[4,3456]{1,0:T(4,128)S(1)} %pad_maximum_fusion.1.mine_ref), channel_id=1, source_target_pairs={{0,4},{1,5},{2,6},{3,7},{4,0},{5,1},{6,2},{7,3},{8,12},{9,13},{10,... | collective-permute-start | bytes 165896 | tf_op jit(solution)/shard_map/ppermute | solution.py:33
